TPU v7x, 32 devices: a whole 2x2x4 slice. The times are simulated.
32 devices in a mesh: grp: 1, deg: 32 (over z, y, x, core).
Axes of the slice: x: 2, y: 2, z: 4, core: 2. Of those that a mesh axis runs over, the one named last changes fastest.
Arguments:
- coeffs_in: float32 [512, 1025, 128], P(('grp', 'deg')), may hold values from -6 to 6
- tables: bfloat16 [512, 1025, 1025], P('deg'), as said below
- order_pairs: int32 [512], replicated, may hold values from 0 to 511, each once
- degree_pairs: int32 [512], replicated, may hold values from 0 to 511, as said below
- angles: float32 [3], replicated, may hold values from -3.140625 to 3.140625
Outputs:
- coeffs_out: float32 [512, 1025, 128], P(('grp', 'deg'))
Inputs may be any that keep to these rules, and one draw needn't show every extreme that they name: `order_pairs`: each pair of orders appears once. `degree_pairs`: each pair of degrees appears once. tables[j] is zero outside its two diagonal blocks: the first degree_pairs[j]+1 rows and columns, and the remaining 1024-degree_pairs[j].
All inputs are finite; a program needn't handle non-finite values.
Results may differ from a plain program's by a relative error of at most 0.005.
Values may be sent and summed in bfloat16 or wider, within the bound.
A program may use at most 192 MiB of HBM per device.

v0:
```python
import jax
import jax.numpy as jnp
from jax import lax
from jax.sharding import PartitionSpec as P


def rotate_phase(values, order_map, angle):
    half = values.shape[-1] // 2
    turn = order_map.astype(jnp.float32)[..., None] * angle
    cosine = jnp.cos(turn)
    sine_part = jnp.sin(turn)
    real_part = values[..., :half].astype(jnp.float32)
    imag_part = values[..., half:].astype(jnp.float32)
    return jnp.concatenate(
        [real_part * cosine + imag_part * sine_part, imag_part * cosine - real_part * sine_part], -1
    )


def packed_places(order_low, degree_low, top):
    lower_side = order_low <= degree_low
    order_pos = jnp.stack(
        [
            top - 1 - degree_low - order_low,
            jnp.where(lower_side, degree_low - order_low, top - degree_low),
        ],
        -1,
    )
    degree_pos = jnp.stack(
        [
            degree_low + 1 + order_low,
            jnp.where(lower_side, order_low, top + degree_low - order_low),
        ],
        -1,
    )
    return (order_pos, degree_pos)


def indicator(places, alive, width):
    columns = jnp.arange(width, dtype=jnp.int32)
    return ((places[..., None] == columns) & alive[..., None]).astype(jnp.bfloat16)


def gather_slots(form, source, places, alive):
    width = source.shape[1]
    pieces = []
    for slot in range(places.shape[-1]):
        table = indicator(places[..., slot], alive[..., slot], width)
        pieces.append(
            jnp.einsum(form, table, source, preferred_element_type=jnp.float32).astype(jnp.bfloat16)
        )
    return jnp.stack(pieces, -2)


def place_slots(form, values, places, alive, width):
    total = None
    for slot in range(places.shape[-1]):
        table = indicator(places[..., slot], alive[..., slot], width)
        term = jnp.einsum(form, table, values[..., slot, :], preferred_element_type=jnp.float32)
        total = term if total is None else total + term
    return total.astype(jnp.bfloat16)


def transform(tables, by_degree, degree_map, tilt):
    first_pass = jnp.einsum("jab,jbc->jac", tables, by_degree, preferred_element_type=jnp.float32)
    tilted = rotate_phase(first_pass, degree_map, tilt).astype(jnp.bfloat16)
    second = jnp.einsum("jab,jbc->jac", tables, tilted, preferred_element_type=jnp.float32)
    return second.astype(jnp.bfloat16)


def shards(coeffs_in, tables, order_pairs, degree_pairs, angles):
    local_pairs, width, channels = coeffs_in.shape
    top = width - 1
    devices = lax.axis_size("deg")
    device = lax.axis_index("deg")
    my_orders = lax.dynamic_slice_in_dim(order_pairs, device * local_pairs, local_pairs)
    my_degrees = lax.dynamic_slice_in_dim(degree_pairs, device * local_pairs, local_pairs)
    all_orders = order_pairs.reshape(devices, local_pairs)
    all_degrees = degree_pairs.reshape(devices, local_pairs)
    position = jnp.arange(width, dtype=jnp.int32)[None, :]
    order_map = jnp.where(
        position < top - my_orders[:, None], my_orders[:, None], top - 1 - my_orders[:, None]
    )
    degree_map = jnp.where(
        position <= my_degrees[:, None], position, position - my_degrees[:, None] - 1
    )
    turned = rotate_phase(coeffs_in, order_map, angles[2]).astype(jnp.bfloat16)
    grid_shape = (devices, local_pairs, local_pairs)
    outward_orders = jnp.broadcast_to(my_orders[None, :, None], grid_shape)
    outward_degrees = jnp.broadcast_to(all_degrees[:, None, :], grid_shape)
    inward_orders = jnp.broadcast_to(all_orders[:, :, None], grid_shape)
    inward_degrees = jnp.broadcast_to(my_degrees[None, None, :], grid_shape)
    out_opos, out_dpos = packed_places(outward_orders, outward_degrees, top)
    in_opos, in_dpos = packed_places(inward_orders, inward_degrees, top)
    out_alive = jnp.ones(out_opos.shape, jnp.bool_)
    in_alive = jnp.ones(in_dpos.shape, jnp.bool_)
    out_found = jnp.any(outward_degrees == outward_orders, axis=-1)
    in_match = inward_degrees == inward_orders
    in_found = jnp.any(in_match, axis=-1)
    in_choice = jnp.argmax(in_match.astype(jnp.int32), axis=-1)
    degree_rows = jnp.arange(local_pairs, dtype=jnp.int32)
    matching = ((in_choice[..., None] == degree_rows) & in_found[..., None]).astype(jnp.bfloat16)
    row_found = jnp.any((in_choice[..., None] == degree_rows) & in_found[..., None], axis=(0, 1))
    extra_places = top - my_orders
    extra_values = jnp.take_along_axis(turned, extra_places[:, None, None], 1)[:, 0]
    main_send = gather_slots("drcw,rwx->drcx", turned, out_opos, out_alive)
    extra_send = jnp.where(out_found[..., None], extra_values[None], 0)
    main_arrived, extra_arrived = (
        lax.all_to_all(main_send, "deg", split_axis=0, concat_axis=0, tiled=True),
        lax.all_to_all(extra_send, "deg", split_axis=0, concat_axis=0, tiled=True),
    )
    by_degree = place_slots("drcw,drcx->cwx", main_arrived, in_dpos, in_alive, width)
    extra_column = jnp.einsum(
        "drq,drx->qx", matching, extra_arrived, preferred_element_type=jnp.float32
    ).astype(jnp.bfloat16)
    by_degree = by_degree.at[:, top].set(
        jnp.where(row_found[:, None], extra_column, by_degree[:, top])
    )
    second = transform(tables, by_degree, degree_map, angles[1])
    main_back = gather_slots("drcw,cwx->drcx", second, in_dpos, in_alive)
    extra_back = jnp.einsum(
        "drq,qx->drx", matching, second[:, top], preferred_element_type=jnp.float32
    ).astype(jnp.bfloat16)
    main_home, extra_home = (
        lax.all_to_all(main_back, "deg", split_axis=0, concat_axis=0, tiled=True),
        lax.all_to_all(extra_back, "deg", split_axis=0, concat_axis=0, tiled=True),
    )
    by_order = place_slots("drcw,drcx->rwx", main_home, out_opos, out_alive, width)
    home_values = jnp.sum(
        jnp.where(out_found[..., None], extra_home.astype(jnp.float32), 0.0), axis=0
    ).astype(jnp.bfloat16)
    home_found = jnp.any(out_found, axis=0)
    home_mask = (position == extra_places[:, None]) & home_found[:, None]
    by_order = jnp.where(home_mask[..., None], home_values[:, None, :], by_order)
    return rotate_phase(by_order, order_map, angles[0])


def solution(mesh):
    return jax.shard_map(
        shards,
        mesh=mesh,
        in_specs=(P(("grp", "deg"), None, None), P("deg", None, None), P(), P(), P()),
        out_specs=P(("grp", "deg"), None, None),
        check_vma=False,
    )
```

profile of v0, /device:TPU:0, one launch (start us, length us, event | category | flops | bytes accessed | tf_op | source)
XLA Modules:
  0.0 439.3 jit_solution(15472936748045340510)
XLA Ops:
  0.0 0.8 broadcast_in_dim.98
  0.8 0.8 compare_and_fusion
  1.6 1.4 fusion.72
  3.0 13.0 %fusion.69 = (f32[16,1025,64]{2,0,1:T(8,128)}, f32[16,1025,64]{2,0,1:T(8,128)}) fusion(f32[16,1025,128]{2,0,1:T(8,128)} %param.7), kind=kLoop, calls=%fused_computation.113 | loop fusion | bytes 16793600 | tf_op jit(solution)/shard_map/slice | solution.py:12
  16.1 2.5 fusion.61
  18.6 9.4 %add_convert_fusion.1 = (bf16[16,1025,64]{2,1,0:T(8,128)(2,1)S(1)}, bf16[16,1025,64]{2,1,0:T(8,128)(2,1)S(1)}) fusion(f32[16,1025,64]{2,0,1:T(8,128)} %get-tuple-element.30, f32[16,1025,64]{2,0,1:T(8,128)} %get-tuple-element.29, f32[16,1025]{1,0:T(8,128)S(1)} %get-tuple-element.44, f32[16,1025]{1,0:T(8,128)S(1)} %get-tuple-element.41), kind=kLoop, calls=%fused_computation.39 | loop fusion | flops 8396800 | bytes 12726400 | tf_op jit(solution)/shard_map/convert.2
  28.0 2.3 pad_maximum_fusion.1
  30.5 7.8 %convert_bitcast_fusion.3 = bf16[32,16,16,1,128]{4,0,2,1,3:T(8,128)(2,1)S(1)} fusion(s32[32,16,16]{0,2,1:T(8,128)S(1)} %get-tuple-element.53, bf16[16,1025,128]{2,1,0:T(8,128)(2,1)S(1)} %pad_maximum_fusion.1), kind=kOutput, calls=%fused_computation.60 | convolution fusion | flops 2159026176 | bytes 6328320 | tf_op jit(solution)/shard_map/drcw,rwx->drcx/dot_general | solution.py:49
  38.4 7.8 %convert_bitcast_fusion.2 = bf16[32,16,16,1,128]{4,0,2,1,3:T(8,128)(2,1)S(1)} fusion(s32[32,16,16]{0,2,1:T(8,128)S(1)} %get-tuple-element.54, bf16[16,1025,128]{2,1,0:T(8,128)(2,1)S(1)} %pad_maximum_fusion.1), kind=kOutput, calls=%fused_computation.59 | convolution fusion | flops 2159026176 | bytes 6328320 | tf_op jit(solution)/shard_map/drcw,rwx->drcx/dot_general | solution.py:49
  46.2 0.4 pad_maximum_fusion.2
  46.6 3.6 copy.61
  50.2 7.9 %all-to-all-start = ((bf16[32,16,16,2,128]{4,2,1,3,0:T(8,128)(2,1)}), bf16[32,16,16,2,128]{4,2,1,3,0:T(8,128)(2,1)}, u32[]{:S(2)}, u32[]{:S(2)}) async-start(bf16[32,16,16,2,128]{4,2,1,3,0:T(8,128)(2,1)} %copy.61), calls=%async_computation | async-start | bytes 8388608 | tf_op jit(solution)/shard_map/all_to_all | solution.py:108
  58.2 8.6 %copy.64 = bf16[16,1025,128]{2,0,1:T(8,128)(2,1)} copy(bf16[16,1025,128]{2,1,0:T(8,128)(2,1)} %copy-done) | data formatting | bytes 8396800 | tf_op jit(solution)/shard_map/concatenate | solution.py:14
  66.8 0.5 compare_reduce_fusion.2
  67.4 0.8 broadcast_add_fusion.1
  68.1 0.7 fusion.53
  69.1 1.3 gather_fusion
  70.5 0.2 fusion.52
  70.8 0.8 broadcast_select_fusion
  71.6 0.1 broadcast_add_fusion
  71.7 0.9 fusion.59
  72.6 79.4 %all-to-all-done = bf16[32,16,16,2,128]{4,2,1,3,0:T(8,128)(2,1)} async-done(((bf16[32,16,16,2,128]{4,2,1,3,0:T(8,128)(2,1)}), bf16[32,16,16,2,128]{4,2,1,3,0:T(8,128)(2,1)}, u32[]{:S(2)}, u32[]{:S(2)}) %all-to-all-start) | async-done | bytes 4194336 | tf_op jit(solution)/shard_map/all_to_all | solution.py:108
  152.0 3.9 all-to-all-start.1
  155.9 3.0 fusion.71
  159.0 13.8 %fusion.1 = f32[16,1025,128,1]{2,1,3,0:T(8,128)} fusion(s32[32,16,16]{0,1,2:T(8,128)S(1)} %get-tuple-element.40, bf16[32,16,16,1,128]{4,2,1,3,0:T(8,128)(2,1)S(1)} %get-tuple-element.36), kind=kOutput, calls=%fused_computation.3 | convolution fusion | flops 2157977600 | bytes 10526720 | tf_op jit(solution)/shard_map/drcw,drcx->cwx/dot_general | solution.py:58
  172.8 14.7 %fusion.23 = bf16[16,1025,128]{2,1,0:T(8,128)(2,1)S(1)} fusion(f32[16,1025,128,1]{2,1,3,0:T(8,128)} %fusion.1, s32[32,16,16]{0,1,2:T(8,128)S(1)} %get-tuple-element.39, bf16[32,16,16,1,128]{4,2,1,3,0:T(8,128)(2,1)S(1)} %get-tuple-element.35), kind=kOutput, calls=%fused_computation.35 | convolution fusion | flops 2162176000 | bytes 14725120 | tf_op jit(solution)/shard_map/drcw,drcx->cwx/dot_general | solution.py:58
  187.5 2.0 copy-done.8
  189.5 0.4 fusion.48
  189.9 0.6 copy_dynamic-update-slice_fusion
  190.6 22.7 %fusion.24 = f32[16,1025,128]{2,1,0:T(8,128)} fusion(bf16[16,1025,128]{2,1,0:T(8,128)(2,1)} %copy_dynamic-update-slice_fusion, bf16[16,1025,1025]{2,0,1:T(8,128)(2,1)} %param.8), kind=kOutput, calls=%fused_computation.40 | convolution fusion | flops 4303360000 | bytes 46215200 | tf_op jit(solution)/shard_map/jab,jbc->jac/dot_general | solution.py:64
  213.2 11.0 %add_convert_fusion = (bf16[16,1025,64]{2,1,0:T(8,128)(2,1)}, bf16[16,1025,64]{2,1,0:T(8,128)(2,1)}) fusion(f32[16,1025,128]{2,1,0:T(8,128)} %fusion.24, f32[16,1025]{1,0:T(8,128)S(1)} %get-tuple-element.46, f32[16,1025]{1,0:T(8,128)S(1)} %get-tuple-element.45), kind=kLoop, calls=%fused_computation.37 | loop fusion | flops 8396800 | bytes 12726400 | tf_op jit(solution)/shard_map/convert
  224.2 24.8 %fusion.27 = bf16[16,128,1025]{1,2,0:T(8,128)(2,1)} fusion(bf16[16,1025,1025]{2,0,1:T(8,128)(2,1)} %param.8, bf16[16,1025,64]{2,1,0:T(8,128)(2,1)} %get-tuple-element.28, bf16[16,1025,64]{2,1,0:T(8,128)(2,1)} %get-tuple-element.27), kind=kOutput, calls=%fused_computation.41 | convolution fusion | flops 4313856000 | bytes 42016800 | tf_op jit(solution)/shard_map/jab,jbc->jac/dot_general | solution.py:66
  249.0 8.3 %convert_bitcast_fusion.1 = bf16[32,16,16,1,128]{4,0,1,2,3:T(8,128)(2,1)S(1)} fusion(s32[32,16,16]{0,1,2:T(8,128)S(1)} %get-tuple-element.39, bf16[16,128,1025]{1,2,0:T(8,128)(2,1)} %fusion.27), kind=kOutput, calls=%fused_computation.58 | convolution fusion | flops 2159026176 | bytes 6328320 | tf_op jit(solution)/shard_map/drcw,cwx->drcx/dot_general | solution.py:49
  257.3 0.8 slice.87
  258.1 1.0 convolution_convert_fusion
  259.0 5.8 %all-to-all-start.2 = ((bf16[32,16,128]{2,1,0:T(8,128)(2,1)}), bf16[32,16,128]{2,1,0:T(8,128)(2,1)S(1)}, u32[]{:S(2)}, u32[]{:S(2)}) async-start(bf16[32,16,128]{2,1,0:T(8,128)(2,1)} %convolution_convert_fusion), calls=%async_computation.2 | async-start | bytes 262144 | tf_op jit(solution)/shard_map/all_to_all | solution.py:125
  264.9 8.3 %convert_bitcast_fusion = bf16[32,16,16,1,128]{4,0,1,2,3:T(8,128)(2,1)S(1)} fusion(s32[32,16,16]{0,1,2:T(8,128)S(1)} %get-tuple-element.40, bf16[16,128,1025]{1,2,0:T(8,128)(2,1)} %fusion.27), kind=kOutput, calls=%fused_computation.57 | convolution fusion | flops 2159026176 | bytes 6328320 | tf_op jit(solution)/shard_map/drcw,cwx->drcx/dot_general | solution.py:49
  273.2 0.4 pad_maximum_fusion.3
  273.6 3.6 copy.69
  277.3 6.2 %all-to-all-start.3 = ((bf16[32,16,16,2,128]{4,1,2,3,0:T(8,128)(2,1)}), bf16[32,16,16,2,128]{4,1,2,3,0:T(8,128)(2,1)}, u32[]{:S(2)}, u32[]{:S(2)}) async-start(bf16[32,16,16,2,128]{4,1,2,3,0:T(8,128)(2,1)} %copy.69), calls=%async_computation.3 | async-start | bytes 8388608 | tf_op jit(solution)/shard_map/all_to_all | solution.py:124
  283.5 0.1 select_reduce_fusion
  283.7 93.7 %all-to-all-done.3 = bf16[32,16,16,2,128]{4,1,2,3,0:T(8,128)(2,1)} async-done(((bf16[32,16,16,2,128]{4,1,2,3,0:T(8,128)(2,1)}), bf16[32,16,16,2,128]{4,1,2,3,0:T(8,128)(2,1)}, u32[]{:S(2)}, u32[]{:S(2)}) %all-to-all-start.3) | async-done | bytes 4194336 | tf_op jit(solution)/shard_map/all_to_all | solution.py:124
  377.4 3.1 fusion.70
  380.5 13.2 %fusion.2 = f32[16,1025,128,1]{2,1,3,0:T(8,128)S(1)} fusion(s32[32,16,16]{0,2,1:T(8,128)S(1)} %get-tuple-element.54, bf16[32,16,16,1,128]{4,1,2,3,0:T(8,128)(2,1)S(1)} %get-tuple-element.34), kind=kOutput, calls=%fused_computation.5 | convolution fusion | flops 2157977600 | bytes 10526720 | tf_op jit(solution)/shard_map/drcw,drcx->rwx/dot_general | solution.py:58
  393.8 16.1 %fusion.30 = bf16[16,1025,128]{2,1,0:T(8,128)(2,1)S(1)} fusion(f32[16,1025,128,1]{2,1,3,0:T(8,128)S(1)} %fusion.2, s32[32,16,16]{0,2,1:T(8,128)S(1)} %copy-done.4, pred[16,1025]{1,0:T(8,128)(4,1)S(1)} %fusion.64, bf16[16,128]{1,0:T(8,128)(2,1)S(1)} %select_reduce_fusion, bf16[32,16,16,1,128]{4,1,2,3,0:T(8,128)(2,1)S(1)} %get-tuple-element.33), kind=kOutput, calls=%fused_computation.42 | convolution fusion | flops 2164275200 | bytes 14745616 | tf_op jit(solution)/shard_map/drcw,drcx->rwx/dot_general | solution.py:58
  410.0 8.0 %fusion.20 = (f32[16,1025,64]{2,1,0:T(8,128)}, f32[16,1025,64]{2,1,0:T(8,128)}) fusion(f32[16,1025]{1,0:T(8,128)S(1)} %copy-done.2, f32[16,1025]{1,0:T(8,128)S(1)} %copy-done.1, bf16[16,1025,128]{2,1,0:T(8,128)(2,1)S(1)} %fusion.30), kind=kLoop, calls=%fused_computation.29 | loop fusion | flops 8396800 | bytes 12726400 | tf_op jit(solution)/shard_map/add | solution.py:15
  417.9 11.3 %pad_maximum_fusion = f32[16,1025,128]{2,1,0:T(8,128)} fusion(f32[16,1025,64]{2,1,0:T(8,128)} %get-tuple-element.32, f32[16,1025,64]{2,1,0:T(8,128)} %get-tuple-element.31), kind=kLoop, calls=%fused_computation.31 | loop fusion | flops 2099200 | bytes 16793600 | tf_op jit(solution)/shard_map/concatenate | solution.py:14
  429.2 9.9 %copy.72 = f32[16,1025,128]{2,0,1:T(8,128)} copy(f32[16,1025,128]{2,1,0:T(8,128)} %pad_maximum_fusion) | data formatting | bytes 16793600 | tf_op jit(solution)/shard_map/concatenate | solution.py:14
  (38 shorter events, 1.0 us)
Async XLA Ops:
  1.6 14.5 %copy-start.5 = (s32[16]{0:T(128)}, s32[16]{0:T(128)S(1)}, u32[]{:S(2)}) copy-start(s32[16]{0:T(128)S(1)} %get-tuple-element.52) | copy-start | bytes 196
  30.4 8.0 %copy-start = (bf16[16,1025,128]{2,1,0:T(8,128)(2,1)}, bf16[16,1025,128]{2,1,0:T(8,128)(2,1)S(1)}, u32[]{:S(2)}) copy-start(bf16[16,1025,128]{2,1,0:T(8,128)(2,1)S(1)} %pad_maximum_fusion.1) | copy-start | bytes 12595204
  30.5 7.9 %copy-start.3 = (s32[32,16,16]{0,2,1:T(8,128)}, s32[32,16,16]{0,2,1:T(8,128)S(1)}, u32[]{:S(2)}) copy-start(s32[32,16,16]{0,2,1:T(8,128)S(1)} %get-tuple-element.53) | copy-start | bytes 98308
  46.6 11.5 %copy-start.7 = (s32[512]{0:T(512)S(1)}, s32[512]{0:T(512)}, u32[]{:S(2)}) copy-start(s32[512]{0:T(512)} %param.9) | copy-start | bytes 6148
  50.2 101.8 %all-to-all-start = ((bf16[32,16,16,2,128]{4,2,1,3,0:T(8,128)(2,1)}), bf16[32,16,16,2,128]{4,2,1,3,0:T(8,128)(2,1)}, u32[]{:S(2)}, u32[]{:S(2)}) async-start(bf16[32,16,16,2,128]{4,2,1,3,0:T(8,128)(2,1)} %copy.61), calls=%async_computation | async-start | bytes 8388608 | tf_op jit(solution)/shard_map/all_to_all | solution.py:108
  152.0 37.5 %all-to-all-start.1 = ((bf16[32,16,128]{2,1,0:T(8,128)(2,1)}), bf16[32,16,128]{2,1,0:T(8,128)(2,1)S(1)}, u32[]{:S(2)}, u32[]{:S(2)}) async-start(bf16[32,16,128]{2,1,0:T(8,128)(2,1)} %broadcast_select_fusion), calls=%async_computation.1 | async-start | bytes 262144 | tf_op jit(solution)/shard_map/all_to_all | solution.py:109
  187.5 2.0 copy-start.8
  259.0 18.2 %all-to-all-start.2 = ((bf16[32,16,128]{2,1,0:T(8,128)(2,1)}), bf16[32,16,128]{2,1,0:T(8,128)(2,1)S(1)}, u32[]{:S(2)}, u32[]{:S(2)}) async-start(bf16[32,16,128]{2,1,0:T(8,128)(2,1)} %convolution_convert_fusion), calls=%async_computation.2 | async-start | bytes 262144 | tf_op jit(solution)/shard_map/all_to_all | solution.py:125
  273.6 9.8 %copy-start.6 = (s32[16]{0:T(128)S(1)}, s32[16]{0:T(128)}, u32[]{:S(2)}) copy-start(s32[16]{0:T(128)} %copy-done.5) | copy-start | bytes 196
  277.3 100.1 %all-to-all-start.3 = ((bf16[32,16,16,2,128]{4,1,2,3,0:T(8,128)(2,1)}), bf16[32,16,16,2,128]{4,1,2,3,0:T(8,128)(2,1)}, u32[]{:S(2)}, u32[]{:S(2)}) async-start(bf16[32,16,16,2,128]{4,1,2,3,0:T(8,128)(2,1)} %copy.69), calls=%async_computation.3 | async-start | bytes 8388608 | tf_op jit(solution)/shard_map/all_to_all | solution.py:124
  380.5 13.2 %copy-start.4 = (s32[32,16,16]{0,2,1:T(8,128)S(1)}, s32[32,16,16]{0,2,1:T(8,128)}, u32[]{:S(2)}) copy-start(s32[32,16,16]{0,2,1:T(8,128)} %copy-done.3) | copy-start | bytes 98308
  393.8 16.2 %copy-start.1 = (f32[16,1025]{1,0:T(8,128)S(1)}, f32[16,1025]{1,0:T(8,128)}, u32[]{:S(2)}) copy-start(f32[16,1025]{1,0:T(8,128)} %get-tuple-element.42) | copy-start | bytes 196804
  393.8 16.2 %copy-start.2 = (f32[16,1025]{1,0:T(8,128)S(1)}, f32[16,1025]{1,0:T(8,128)}, u32[]{:S(2)}) copy-start(f32[16,1025]{1,0:T(8,128)} %get-tuple-element.43) | copy-start | bytes 196804
where the time goes:
time: 447 us; the launch traced here: 439 us
  waiting for transfers between devices  173 us (39%)
  matrix products  139 us (31%)
  local copies, waits for them, and re-layouts  52.4 us (12%)
  other arithmetic  50.4 us (11%)
  starting transfers between devices  23.8 us (5%)
    all_to_all x1, waiting for transfers between devices, shards(): lax.all_to_all(main_back, 'deg', split_axis=0, concat_axis=0, tiled=True)  93.7 us
    all_to_all x1, waiting for transfers between devices, shards(): lax.all_to_all(main_send, 'deg', split_axis=0, concat_axis=0, tiled=True)  79.4 us
    dot_general x4, matrix products, place_slots(): jnp.einsum(form, table, values[..., slot, :], preferred_element_type=jnp....  57.9 us
    dot_general x4, matrix products, gather_slots(): jnp.einsum(form, table, source, preferred_element_type=jnp.float32)  32.4 us
    dot_general x1, matrix products, transform(): jnp.einsum('jab,jbc->jac', tables, tilted, preferred_element_type=jnp.flo...  24.8 us
    dot_general x1, matrix products, transform(): jnp.einsum('jab,jbc->jac', tables, by_degree, preferred_element_type=jnp....  22.7 us
    another operation x2, other arithmetic  20.4 us
    concatenate x2, local copies, waits for them, and re-layouts, rotate_phase(): jnp.concatenate([real_part * cosine + imag_part * sine_part, imag_part *...  18.5 us
  transfers between devices with their start and end apart: 4, of which 2 were waited for; matrix products, arithmetic and copies ran while one was open for 13% of the time, Pallas kernels for 0%

commit v1 on v0

--- a/solution.py
+++ b/solution.py
@@ -1,6 +1,10 @@
+import functools
+
 import jax
 import jax.numpy as jnp
 from jax import lax
+from jax.experimental import pallas as pl
+from jax.experimental.pallas import tpu as pltpu
 from jax.sharding import PartitionSpec as P
 
 
@@ -67,7 +71,7 @@
     return second.astype(jnp.bfloat16)
 
 
-def shards(coeffs_in, tables, order_pairs, degree_pairs, angles):
+def small_shards(coeffs_in, tables, order_pairs, degree_pairs, angles):
     local_pairs, width, channels = coeffs_in.shape
     top = width - 1
     devices = lax.axis_size("deg")
@@ -134,6 +138,279 @@
     return rotate_phase(by_order, order_map, angles[0])
 
 
+CHUNKS = 2
+VMEM = pl.BlockSpec(memory_space=pltpu.VMEM)
+SMEM = pl.BlockSpec(memory_space=pltpu.SMEM)
+ANY = pl.BlockSpec(memory_space=pl.ANY)
+F32 = jnp.float32
+BF16 = jnp.bfloat16
+
+
+def onehot(a, b):
+    return jnp.where(a == b, 1.0, 0.0).astype(BF16)
+
+
+def rotate(v, cosine, sine):
+    return v * cosine + pltpu.roll(v, v.shape[-1] // 2, v.ndim - 1) * sine
+
+
+def dot(a, b):
+    return jnp.dot(a, b, preferred_element_type=F32)
+
+
+def iota(shape, dim):
+    return lax.broadcasted_iota(jnp.int32, shape, dim)
+
+
+def pack_kernel(local, pairs, chunks, ord_ref, x_ref, qcol_ref, cs_ref, *rest):
+    outs = rest[:chunks]
+    xs, scr0, scr1, extra, q0, q1, sem = rest[chunks:]
+    width = 2 * pairs + 1
+    devices = pairs // local
+    each = local // chunks
+    copy = pltpu.make_async_copy(x_ref, xs.at[pl.ds(pairs * local, width * local)], sem)
+    copy.start()
+    column = iota((pairs, pairs), 1)
+    q0[...] = onehot(column, pairs - 1 - qcol_ref[...])
+    q1[...] = onehot(column, qcol_ref[...])
+    copy.wait()
+    row = iota((pairs, 1), 0)
+
+    def step(r, carry):
+        p = ord_ref[r]
+        cl, sl, ch, sh = (cs_ref[i, pl.ds(r, 1), :] for i in range(4))
+
+        def load(pos):
+            return xs[pl.ds((pairs + pos) * local + r, pairs, stride=local), :]
+
+        low = jnp.where(row >= p, rotate(load(-p), cl, sl), 0.0).astype(BF16)
+        mid = rotate(load(pairs - p), cl, sl).astype(BF16)
+        high = jnp.where(row >= pairs - p, rotate(load(pairs + 1), ch, sh), 0.0).astype(BF16)
+        both = dot(q0[...], jnp.concatenate([mid, high], 1))
+        scr0[pl.ds(r, pairs, stride=local), :] = both[:, :128]
+        scr1[pl.ds(r, pairs, stride=local), :] = both[:, 128:] + dot(q1[...], low)
+        extra[pl.ds(r, 1), :] = rotate(xs[pl.ds((pairs + width - 1 - p) * local + r, 1), :], ch, sh)
+        return carry
+
+    lax.fori_loop(0, local, step, 0)
+    span = each * local
+
+    def emit(d, carry):
+        for k, out in enumerate(outs):
+            at = pl.multiple_of(d * local * local + k * span, 16)
+            out[d, 0:span, :] = scr0[pl.ds(at, span), :].astype(BF16)
+            out[d, span : 2 * span, :] = scr1[pl.ds(at, span), :].astype(BF16)
+        outs[0][d, 2 * span :, :] = extra[...].astype(BF16)
+        return carry
+
+    lax.fori_loop(0, devices, emit, 0)
+
+
+def degree_kernel(local, pairs, each, last, deg_ref, recv, ein, eprev, prow, pcol, ct, st, table, *rest):
+    if last:
+        out, a0, arev, a0t, arevt, buf, eacc = rest
+    else:
+        out, eout, a0, arev, a0t, arevt, buf, eacc = rest
+    width = 2 * pairs + 1
+    devices = pairs // local
+    c = pl.program_id(0)
+
+    @pl.when(c == 0)
+    def _():
+        r0 = iota((pairs, pairs), 0)
+        r1 = iota((pairs, pairs), 1)
+        a0[...] = onehot(r0, prow[...])
+        arev[...] = onehot(pairs - 1 - r0, prow[...])
+        a0t[...] = onehot(r1, pcol[...])
+        arevt[...] = onehot(pairs - 1 - r1, pcol[...])
+        eacc[...] = eprev[...]
+
+    q = deg_ref[c]
+    at0 = pl.multiple_of(c * local, 16)
+    at1 = pl.multiple_of((each + c) * local, 16)
+    in0 = recv[:, pl.ds(at0, local), :].reshape(pairs, 128)
+    in1 = recv[:, pl.ds(at1, local), :].reshape(pairs, 128)
+    u = dot(a0[...], jnp.concatenate([in0, in1], 1))
+    v = dot(arev[...], in1)
+    pick = onehot(jnp.broadcast_to(prow[...], (8, pairs)), q)
+    e = dot(pick, ein[...].reshape(pairs, 128))
+    buf[0:pairs, :] = u[:, 128:]
+    buf[pl.ds(q + 1, pairs), :] = u[:, :128]
+    buf[pl.ds(q + 1 + pairs, pairs), :] = v
+    buf[width - 1 : width, :] = e[0:1]
+    first = dot(table[...], buf[0:width, :].astype(BF16))
+    low = iota((width, 1), 0) <= q
+    cosine = jnp.where(low, ct[pairs : pairs + width, :], ct[pl.ds(pairs - 1 - q, width), :])
+    sine = jnp.where(low, st[pairs : pairs + width, :], st[pl.ds(pairs - 1 - q, width), :])
+    tilted = rotate(first, cosine, sine).astype(BF16)
+    buf[0:width, :] = dot(table[...], tilted).astype(BF16).astype(F32)
+    row = iota((pairs, 1), 0)
+    f0 = buf[pl.ds(q + 1, pairs), :].astype(BF16)
+    f1 = jnp.where(row <= q, buf[0:pairs, :], 0.0).astype(BF16)
+    back = jnp.where(row < pairs - 1 - q, buf[pl.ds(q + 1 + pairs, pairs), :], 0.0).astype(BF16)
+    g = dot(a0t[...], jnp.concatenate([f0, f1], 1))
+    h = g[:, 128:] + dot(arevt[...], back)
+    out[:, pl.ds(at0, local), :] = g[:, :128].astype(BF16).reshape(devices, local, 128)
+    out[:, pl.ds(at1, local), :] = h.astype(BF16).reshape(devices, local, 128)
+    eacc[...] += jnp.where(pcol[...] == q, buf[width - 1 : width, :], 0.0)
+
+    @pl.when(c == each - 1)
+    def _():
+        if last:
+            out[:, 2 * each * local :, :] = eacc[...].astype(BF16).reshape(devices, local, 128)
+        else:
+            eout[...] = eacc[...]
+
+
+def unpack_kernel(local, pairs, chunks, ord_ref, qrow_ref, cs_ref, *rest):
+    backs = rest[:chunks]
+    out_ref, os, scr0, scr1, extra, q0, q1, sem = rest[chunks:]
+    width = 2 * pairs + 1
+    devices = pairs // local
+    each = local // chunks
+    span = each * local
+    extra[...] = jnp.zeros(extra.shape, F32)
+
+    def take(d, carry):
+        for k, back in enumerate(backs):
+            at = pl.multiple_of(d * local * local + k * span, 16)
+            scr0[pl.ds(at, span), :] = back[d, 0:span, :].astype(F32)
+            scr1[pl.ds(at, span), :] = back[d, span : 2 * span, :].astype(F32)
+        extra[...] += backs[-1][d, 2 * span :, :].astype(F32)
+        return carry
+
+    lax.fori_loop(0, devices, take, 0)
+    row = iota((pairs, pairs), 0)
+    q0[...] = onehot(pairs - 1 - row, qrow_ref[...])
+    q1[...] = onehot(row, qrow_ref[...])
+
+    def step(r, carry):
+        p = ord_ref[r]
+        cl, sl, ch, sh = (cs_ref[i, pl.ds(r, 1), :] for i in range(4))
+        s0 = scr0[pl.ds(r, pairs, stride=local), :].astype(BF16)
+        s1 = scr1[pl.ds(r, pairs, stride=local), :].astype(BF16)
+        both = dot(q0[...], jnp.concatenate([s0, s1], 1))
+        low = dot(q1[...], s1)
+
+        def put(pos, value):
+            os[pl.ds((pairs + pos) * local + r, pairs, stride=local), :] = value
+
+        put(pairs + 1, rotate(both[:, 128:], ch, sh))
+        put(-p, rotate(low, cl, sl))
+        put(pairs - p, rotate(both[:, :128], cl, sl))
+        os[pl.ds((pairs + width - 1 - p) * local + r, 1), :] = rotate(extra[pl.ds(r, 1), :], ch, sh)
+        return carry
+
+    lax.fori_loop(0, local, step, 0)
+    copy = pltpu.make_async_copy(os.at[pl.ds(pairs * local, width * local)], out_ref, sem)
+    copy.start()
+    copy.wait()
+
+
+def phases(orders, angle):
+    turn = orders.astype(F32) * angle
+    cosine, sine = jnp.cos(turn), jnp.sin(turn)
+    lane = jnp.arange(128) < 64
+    return (
+        jnp.broadcast_to(cosine[:, None], (orders.shape[0], 128)),
+        jnp.where(lane[None, :], sine[:, None], -sine[:, None]),
+    )
+
+
+def shards(coeffs_in, tables, order_pairs, degree_pairs, angles):
+    local, width, channels = coeffs_in.shape
+    top = width - 1
+    pairs = top // 2
+    if local % 16 or channels != 128 or pairs % 128:
+        return small_shards(coeffs_in, tables, order_pairs, degree_pairs, angles)
+    chunks = CHUNKS
+    each = local // chunks
+    devices = lax.axis_size("deg")
+    device = lax.axis_index("deg")
+    my_orders = lax.dynamic_slice_in_dim(order_pairs, device * local, local)
+    my_degrees = lax.dynamic_slice_in_dim(degree_pairs, device * local, local)
+    params = pltpu.CompilerParams(vmem_limit_bytes=56 * 1024 * 1024)
+    turn_in = jnp.stack(phases(my_orders, angles[2]) + phases(top - 1 - my_orders, angles[2]))
+    turn_out = jnp.stack(phases(my_orders, angles[0]) + phases(top - 1 - my_orders, angles[0]))
+    ct, st = (
+        jnp.pad(t, ((pairs, 7), (0, 0))) for t in phases(jnp.arange(width, dtype=jnp.int32), angles[1])
+    )
+    flat = jnp.transpose(coeffs_in, (1, 0, 2)).reshape(width * local, channels)
+    main_rows = 2 * each * local
+    rows = [main_rows + (local if k == 0 else 0) for k in range(chunks)]
+    back_rows = [main_rows + (local if k == chunks - 1 else 0) for k in range(chunks)]
+    square = pltpu.VMEM((pairs, pairs), BF16)
+    slots = pltpu.VMEM((pairs * local, 128), F32)
+    line = pltpu.VMEM(((pairs + width) * local, 128), F32)
+    sends = pl.pallas_call(
+        functools.partial(pack_kernel, local, pairs, chunks),
+        name="pack",
+        out_shape=[jax.ShapeDtypeStruct((devices, n, 128), BF16) for n in rows],
+        in_specs=[SMEM, ANY, VMEM, VMEM],
+        out_specs=[VMEM] * chunks,
+        scratch_shapes=[line, slots, slots, pltpu.VMEM((local, 128), F32), square, square, pltpu.SemaphoreType.DMA],
+        compiler_params=params,
+        cost_estimate=pl.CostEstimate(flops=6 * 10**9, bytes_accessed=13 * 10**6, transcendentals=0),
+    )(my_orders, flat, degree_pairs[:, None], turn_in)
+    swap = functools.partial(lax.all_to_all, axis_name="deg", split_axis=0, concat_axis=0, tiled=True)
+    arrived = [swap(s) for s in sends]
+    extra_in = arrived[0][:, main_rows:, :]
+    extra_back = jnp.zeros((pairs, 128), F32)
+    homes = []
+    for k in range(chunks):
+        last = k == chunks - 1
+        full2 = lambda c, deg: (0, 0)
+        full3 = lambda c, deg: (0, 0, 0)
+        out_shape = [jax.ShapeDtypeStruct((devices, back_rows[k], 128), BF16)]
+        out_specs = [pl.BlockSpec((devices, back_rows[k], 128), full3)]
+        if not last:
+            out_shape.append(jax.ShapeDtypeStruct((pairs, 128), F32))
+            out_specs.append(pl.BlockSpec((pairs, 128), full2))
+        done = pl.pallas_call(
+            functools.partial(degree_kernel, local, pairs, each, last),
+            name="degree",
+            out_shape=out_shape,
+            grid_spec=pltpu.PrefetchScalarGridSpec(
+                num_scalar_prefetch=1,
+                grid=(each,),
+                in_specs=[
+                    pl.BlockSpec((devices, rows[k], 128), full3),
+                    pl.BlockSpec((devices, local, 128), full3),
+                    pl.BlockSpec((pairs, 128), full2),
+                    pl.BlockSpec((1, pairs), full2),
+                    pl.BlockSpec((pairs, 1), full2),
+                    pl.BlockSpec(ct.shape, full2),
+                    pl.BlockSpec(st.shape, full2),
+                    pl.BlockSpec((None, width, width), lambda c, deg, k=k: (k * each + c, 0, 0)),
+                ],
+                out_specs=out_specs,
+                scratch_shapes=[square] * 4
+                + [pltpu.VMEM((3 * pairs + 16, 128), F32), pltpu.VMEM((pairs, 128), F32)],
+            ),
+            compiler_params=params,
+            cost_estimate=pl.CostEstimate(
+                flops=16 * 10**9 // chunks, bytes_accessed=50 * 10**6 // chunks, transcendentals=0
+            ),
+        )(
+            my_degrees[k * each : (k + 1) * each], arrived[k], extra_in, extra_back,
+            order_pairs[None, :], order_pairs[:, None], ct, st, tables,
+        )
+        if not last:
+            extra_back = done[1]
+        homes.append(swap(done[0]))
+    result = pl.pallas_call(
+        functools.partial(unpack_kernel, local, pairs, chunks),
+        name="unpack",
+        out_shape=jax.ShapeDtypeStruct((width * local, 128), F32),
+        in_specs=[SMEM, VMEM, VMEM] + [VMEM] * chunks,
+        out_specs=ANY,
+        scratch_shapes=[line, slots, slots, pltpu.VMEM((local, 128), F32), square, square, pltpu.SemaphoreType.DMA],
+        compiler_params=params,
+        cost_estimate=pl.CostEstimate(flops=6 * 10**9, bytes_accessed=13 * 10**6, transcendentals=0),
+    )(my_orders, degree_pairs[None, :], turn_out, *homes)
+    return jnp.transpose(result.reshape(width, local, 128), (1, 0, 2))
+
+
 def solution(mesh):
     return jax.shard_map(
         shards,

time: 447 us -> 300 us (0.67); the launches traced: 439 us -> 300 us
  matrix products: 139 us -> 0 us
  Pallas kernels: 0 us -> 120 us
  waiting for transfers between devices: 173 us -> 62.9 us
  blocking collectives: 0 us -> 60.4 us
  other arithmetic: 50.4 us -> 5.54 us
  local copies, waits for them, and re-layouts: 52.4 us -> 37.7 us
  starting transfers between devices: 23.8 us -> 13.3 us
    dot_general x12 -> x0, matrix products: 139 us -> none  [the longest x4 57.9 us: place_slots(): jnp.einsum(form, table, values[..., slot, :], preferred_element_type=jnp....]
    pallas_call x0 -> x4, Pallas kernels: none -> 120 us  [the longest x2 74.1 us: shards(): pl.pallas_call(functools.partial(degree_kernel, local, pairs, each, last)...]
    all_to_all x4 -> x3, waiting for transfers between devices: 173 us -> 62.9 us  [the longest x2 62.9 us: shards(): homes.append(swap(done[0]))]
    all_to_all x0 -> x1, blocking collectives: none -> 60.4 us  [shards(): arrived = [swap(s) for s in sends]]
    unnamed x19 -> x11, local copies, waits for them, and re-layouts: 2.06 us -> 28.8 us
    another operation x5 -> x2, other arithmetic: 21.9 us -> 1.25 us  [the longest x1 0.62 us: shards(): jnp.stack(phases(my_orders, angles[2]) + phases(top - 1 - my_orders, angl...]
    slice x6 -> x3, local copies, waits for them, and re-layouts: 21.3 us -> 2.67 us  [the longest x1 1.35 us: shards(): angles[1]]
    concatenate x2 -> x0, local copies, waits for them, and re-layouts: 18.5 us -> none  [rotate_phase(): jnp.concatenate([real_part * cosine + imag_part * sine_part, imag_part *...]
  transfers between devices with their start and end apart: 4 -> 3, of which waited for: 2 -> 2; matrix products, arithmetic and copies ran while one was open for 13% -> 11% of each run, Pallas kernels for 0% -> 25%
where the time goes in v1:
time: 300 us
  Pallas kernels  120 us (40%)
  waiting for transfers between devices  62.9 us (21%)
  blocking collectives  60.4 us (20%)
  local copies, waits for them, and re-layouts  37.7 us (13%)
  starting transfers between devices  13.3 us (4%)
  other arithmetic  5.54 us (2%)
    pallas_call x2, Pallas kernels, shards(): pl.pallas_call(functools.partial(degree_kernel, local, pairs, each, last)...  74.1 us
    all_to_all x2, waiting for transfers between devices, shards(): homes.append(swap(done[0]))  62.9 us
    all_to_all x1, blocking collectives, shards(): arrived = [swap(s) for s in sends]  60.4 us
    unnamed x11, local copies, waits for them, and re-layouts  28.8 us
    pallas_call x1, Pallas kernels, shards(): pl.pallas_call(functools.partial(unpack_kernel, local, pairs, chunks), na...  23.4 us
    pallas_call x1, Pallas kernels, shards(): pl.pallas_call(functools.partial(pack_kernel, local, pairs, chunks), name...  22.1 us
    all_to_all x2, starting transfers between devices, shards(): homes.append(swap(done[0]))  9.69 us
  transfers between devices with their start and end apart: 3, of which 2 were waited for; matrix products, arithmetic and copies ran while one was open for 11% of the time, Pallas kernels for 25%

profile of v1, /device:TPU:0, one launch (start us, length us, event | category | flops | bytes accessed | tf_op | source)
XLA Modules:
  0.0 299.5 jit_solution(6751206164288198298)
XLA Ops:
  0.0 1.4 fusion.20
  1.4 1.5 copy.8.qcol_ref
  2.9 1.4 fusion.6
  4.3 0.0 copy-start.4
  4.3 1.3 fusion.11
  5.5 0.1 broadcast_select_fusion.2
  5.6 0.1 stack_broadcast_in_dim.11
  5.7 0.1 stack_broadcast_in_dim.10
  5.8 0.6 pad_maximum_fusion.1.cs_ref
  6.4 0.0 copy-done.4
  6.4 22.1 %pack.1 = (bf16[32,272,128]{2,1,0:T(8,128)(2,1)}, bf16[32,256,128]{2,1,0:T(8,128)(2,1)}) custom-call(s32[16]{0:T(128)} %copy-done.4, f32[16400,128]{1,0:T(8,128)} %bitcast.18, s32[512,1]{1,0:T(8,128)} %copy.8.qcol_ref, f32[4,16,128]{2,1,0:T(8,128)} %pad_maximum_fusion.1.cs_ref), custom_call_target="tpu_custom_call" | custom-call | flops 6000000000 | bytes 13000000 | tf_op jit(solution)/shard_map/pack/pallas_call | solution.py:345
  28.5 60.4 %all_to_all.20.recv = bf16[32,272,128]{2,1,0:T(8,128)(2,1)S(1)} all-to-all(bf16[32,272,128]{2,1,0:T(8,128)(2,1)} %get-tuple-element.9), channel_id=1, replica_groups=mesh['grp'=1,'deg'=32] {'deg'}, dimensions={0} | all-to-all | bytes 4456448 | tf_op jit(solution)/shard_map/all_to_all | solution.py:356
  88.9 0.0 copy-start
  89.0 3.6 %all-to-all-start.2 = ((bf16[32,256,128]{2,1,0:T(8,128)(2,1)}), bf16[32,256,128]{2,1,0:T(8,128)(2,1)}, u32[]{:S(2)}, u32[]{:S(2)}) async-start(bf16[32,256,128]{2,1,0:T(8,128)(2,1)} %get-tuple-element.11), calls=%async_computation.2 | async-start | bytes 4194304 | tf_op jit(solution)/shard_map/all_to_all | solution.py:356
  92.5 0.8 dynamic_slice.7
  93.3 0.6 fusion.2
  93.9 0.6 fusion
  94.5 0.3 broadcast_select_fusion
  94.9 0.9 pad.11.st
  95.8 0.0 copy-start.3
  95.8 26.1 %copy.10.table = bf16[16,1025,1025]{2,1,0:T(8,128)(2,1)} copy(bf16[16,1025,1025]{2,0,1:T(8,128)(2,1)} %param.6) | data formatting | bytes 67240000 | tf_op args[1]
  121.9 0.0 copy-done.3
  121.9 0.9 copy.9.pcol
  122.8 0.6 fusion.19
  123.4 0.0 copy-done
  123.4 0.7 slice.26.ein
  124.1 1.1 pad.10.ct
  125.2 0.7 broadcast_in_dim.144.eprev
  126.0 37.1 %degree.2 = (bf16[32,256,128]{2,1,0:T(8,128)(2,1)}, f32[512,128]{1,0:T(8,128)}) custom-call(s32[8]{0:T(128)} %get-tuple-element.24.deg_ref, bf16[32,272,128]{2,1,0:T(8,128)(2,1)} %copy-done, bf16[32,16,128]{2,1,0:T(8,128)(2,1)} %slice.26.ein, f32[512,128]{1,0:T(8,128)} %broadcast_in_dim.144.eprev, s32[1,512]{1,0:T(1,128)} %bitcast.13, s32[512,1]{1,0:T(8,128)} %copy.9.pcol, ...), custom_call_target="tpu_custom_call" | custom-call | flops 8000000000 | bytes 25000000 | tf_op jit(solution)/shard_map/degree/pallas_call | solution.py:369
  163.1 0.0 all-to-all-done.2.recv
  163.1 5.7 %all-to-all-start.1 = ((bf16[32,256,128]{2,1,0:T(8,128)(2,1)}), bf16[32,256,128]{2,1,0:T(8,128)(2,1)S(1)}, u32[]{:S(2)}, u32[]{:S(2)}) async-start(bf16[32,256,128]{2,1,0:T(8,128)(2,1)} %get-tuple-element.10), calls=%async_computation.1 | async-start | bytes 4194304 | tf_op jit(solution)/shard_map/all_to_all | solution.py:400
  168.8 37.0 %degree.3 = bf16[32,272,128]{2,1,0:T(8,128)(2,1)} custom-call(s32[8]{0:T(128)} %get-tuple-element.23.deg_ref, bf16[32,256,128]{2,1,0:T(8,128)(2,1)} %all-to-all-done.2.recv, bf16[32,16,128]{2,1,0:T(8,128)(2,1)} %slice.26.ein, f32[512,128]{1,0:T(8,128)} %get-tuple-element.12.eprev, s32[1,512]{1,0:T(1,128)} %bitcast.14, s32[512,1]{1,0:T(8,128)} %copy.9.pcol, ...), custom_call_target="tpu_custom_call" | custom-call | flops 8000000000 | bytes 25000000 | tf_op jit(solution)/shard_map/degree/pallas_call | solution.py:369
  205.8 11.9 %all-to-all-done.1.rest_0_ = bf16[32,256,128]{2,1,0:T(8,128)(2,1)S(1)} async-done(((bf16[32,256,128]{2,1,0:T(8,128)(2,1)}), bf16[32,256,128]{2,1,0:T(8,128)(2,1)S(1)}, u32[]{:S(2)}, u32[]{:S(2)}) %all-to-all-start.1) | async-done | bytes 2097184 | tf_op jit(solution)/shard_map/all_to_all | solution.py:400
  217.7 0.0 copy-start.2
  217.7 1.3 copy-done.2
  219.0 4.0 %all-to-all-start.3 = ((bf16[32,272,128]{2,1,0:T(8,128)(2,1)}), bf16[32,272,128]{2,1,0:T(8,128)(2,1)S(1)}, u32[]{:S(2)}, u32[]{:S(2)}) async-start(bf16[32,272,128]{2,1,0:T(8,128)(2,1)} %degree.3), calls=%async_computation.3 | async-start | bytes 4456448 | tf_op jit(solution)/shard_map/all_to_all | solution.py:400
  223.0 0.1 stack_broadcast_in_dim.8
  223.1 0.1 stack_broadcast_in_dim.9
  223.1 0.6 pad_maximum_fusion.cs_ref
  223.8 51.0 %all-to-all-done.3.rest_1_ = bf16[32,272,128]{2,1,0:T(8,128)(2,1)S(1)} async-done(((bf16[32,272,128]{2,1,0:T(8,128)(2,1)}), bf16[32,272,128]{2,1,0:T(8,128)(2,1)S(1)}, u32[]{:S(2)}, u32[]{:S(2)}) %all-to-all-start.3) | async-done | bytes 2228256 | tf_op jit(solution)/shard_map/all_to_all | solution.py:400
  274.7 0.0 copy-start.1
  274.7 1.4 copy-done.1
  276.1 23.4 %unpack.1 = f32[16400,128]{1,0:T(8,128)} custom-call(s32[16]{0:T(128)} %copy-done.4, s32[1,512]{1,0:T(1,128)} %bitcast.17, f32[4,16,128]{2,1,0:T(8,128)} %pad_maximum_fusion.cs_ref, bf16[32,256,128]{2,1,0:T(8,128)(2,1)} %copy-done.2, bf16[32,272,128]{2,1,0:T(8,128)(2,1)} %copy-done.1), custom_call_target="tpu_custom_call" | custom-call | flops 6000000000 | bytes 13000000 | tf_op jit(solution)/shard_map/unpack/pallas_call | solution.py:401
  (2 shorter events, 0.0 us)
Async XLA Ops:
  4.3 2.2 copy-start.4
  88.9 34.5 %copy-start = (bf16[32,272,128]{2,1,0:T(8,128)(2,1)}, bf16[32,272,128]{2,1,0:T(8,128)(2,1)S(1)}, u32[]{:S(2)}) copy-start(bf16[32,272,128]{2,1,0:T(8,128)(2,1)S(1)} %all_to_all.20.recv) | copy-start | bytes 6684676
  89.0 74.2 %all-to-all-start.2 = ((bf16[32,256,128]{2,1,0:T(8,128)(2,1)}), bf16[32,256,128]{2,1,0:T(8,128)(2,1)}, u32[]{:S(2)}, u32[]{:S(2)}) async-start(bf16[32,256,128]{2,1,0:T(8,128)(2,1)} %get-tuple-element.11), calls=%async_computation.2 | async-start | bytes 4194304 | tf_op jit(solution)/shard_map/all_to_all | solution.py:356
  95.8 26.1 %copy-start.3 = (s32[512]{0:T(512)S(1)}, s32[512]{0:T(512)}, u32[]{:S(2)}) copy-start(s32[512]{0:T(512)} %param.7) | copy-start | bytes 6148
  163.1 54.6 %all-to-all-start.1 = ((bf16[32,256,128]{2,1,0:T(8,128)(2,1)}), bf16[32,256,128]{2,1,0:T(8,128)(2,1)S(1)}, u32[]{:S(2)}, u32[]{:S(2)}) async-start(bf16[32,256,128]{2,1,0:T(8,128)(2,1)} %get-tuple-element.10), calls=%async_computation.1 | async-start | bytes 4194304 | tf_op jit(solution)/shard_map/all_to_all | solution.py:400
  217.7 1.3 copy-start.2
  219.0 55.7 %all-to-all-start.3 = ((bf16[32,272,128]{2,1,0:T(8,128)(2,1)}), bf16[32,272,128]{2,1,0:T(8,128)(2,1)S(1)}, u32[]{:S(2)}, u32[]{:S(2)}) async-start(bf16[32,272,128]{2,1,0:T(8,128)(2,1)} %degree.3), calls=%async_computation.3 | async-start | bytes 4456448 | tf_op jit(solution)/shard_map/all_to_all | solution.py:400
  274.7 1.4 copy-start.1

commit v2 on v1

--- a/solution.py
+++ b/solution.py
@@ -4,6 +4,7 @@
 import jax.numpy as jnp
 from jax import lax
 from jax.experimental import pallas as pl
+from jax.experimental.layout import Layout, with_layout_constraint
 from jax.experimental.pallas import tpu as pltpu
 from jax.sharding import PartitionSpec as P
 
@@ -139,6 +140,7 @@
 
 
 CHUNKS = 2
+HALVES = 2
 VMEM = pl.BlockSpec(memory_space=pltpu.VMEM)
 SMEM = pl.BlockSpec(memory_space=pltpu.SMEM)
 ANY = pl.BlockSpec(memory_space=pl.ANY)
@@ -162,14 +164,17 @@
     return lax.broadcasted_iota(jnp.int32, shape, dim)
 
 
-def pack_kernel(local, pairs, chunks, ord_ref, x_ref, qcol_ref, cs_ref, *rest):
+def pack_kernel(half, pairs, chunks, ord_ref, x_ref, qcol_ref, cs_ref, *rest):
     outs = rest[:chunks]
-    xs, scr0, scr1, extra, q0, q1, sem = rest[chunks:]
+    xs3, scr0, scr1, extra, q0, q1, sem = rest[chunks:]
+    part = cs_ref.shape[1]
     width = 2 * pairs + 1
-    devices = pairs // local
-    each = local // chunks
-    copy = pltpu.make_async_copy(x_ref, xs.at[pl.ds(pairs * local, width * local)], sem)
+    devices, each = outs[0].shape[0], outs[1].shape[1] // 2
+    copy = pltpu.make_async_copy(
+        x_ref.at[:, pl.ds(half * part, part), :], xs3.at[pl.ds(pairs, width)], sem
+    )
     copy.start()
+    xs = xs3.reshape((pairs + width) * part, 128)
     column = iota((pairs, pairs), 1)
     q0[...] = onehot(column, pairs - 1 - qcol_ref[...])
     q1[...] = onehot(column, qcol_ref[...])
@@ -181,38 +186,47 @@
         cl, sl, ch, sh = (cs_ref[i, pl.ds(r, 1), :] for i in range(4))
 
         def load(pos):
-            return xs[pl.ds((pairs + pos) * local + r, pairs, stride=local), :]
+            return xs[pl.ds((pairs + pos) * part + r, pairs, stride=part), :]
 
         low = jnp.where(row >= p, rotate(load(-p), cl, sl), 0.0).astype(BF16)
         mid = rotate(load(pairs - p), cl, sl).astype(BF16)
         high = jnp.where(row >= pairs - p, rotate(load(pairs + 1), ch, sh), 0.0).astype(BF16)
         both = dot(q0[...], jnp.concatenate([mid, high], 1))
-        scr0[pl.ds(r, pairs, stride=local), :] = both[:, :128]
-        scr1[pl.ds(r, pairs, stride=local), :] = both[:, 128:] + dot(q1[...], low)
-        extra[pl.ds(r, 1), :] = rotate(xs[pl.ds((pairs + width - 1 - p) * local + r, 1), :], ch, sh)
+        scr0[pl.ds(r, pairs, stride=part), :] = both[:, :128]
+        scr1[pl.ds(r, pairs, stride=part), :] = both[:, 128:] + dot(q1[...], low)
+        extra[pl.ds(r, 1), :] = rotate(xs[pl.ds((pairs + width - 1 - p) * part + r, 1), :], ch, sh)
         return carry
 
-    lax.fori_loop(0, local, step, 0)
-    span = each * local
+    lax.fori_loop(0, part, step, 0)
+    span = each * part
 
     def emit(d, carry):
         for k, out in enumerate(outs):
-            at = pl.multiple_of(d * local * local + k * span, 16)
-            out[d, 0:span, :] = scr0[pl.ds(at, span), :].astype(BF16)
-            out[d, span : 2 * span, :] = scr1[pl.ds(at, span), :].astype(BF16)
-        outs[0][d, 2 * span :, :] = extra[...].astype(BF16)
+            at = pl.multiple_of((d * chunks + k) * span, 8)
+            out[d, 0:each] = scr0[pl.ds(at, span), :].reshape(each, part, 128).astype(BF16)
+            out[d, each : 2 * each] = scr1[pl.ds(at, span), :].reshape(each, part, 128).astype(BF16)
+        outs[0][d, 2 * each] = extra[...].astype(BF16)
         return carry
 
     lax.fori_loop(0, devices, emit, 0)
 
 
-def degree_kernel(local, pairs, each, last, deg_ref, recv, ein, eprev, prow, pcol, ct, st, table, *rest):
-    if last:
-        out, a0, arev, a0t, arevt, buf, eacc = rest
-    else:
-        out, eout, a0, arev, a0t, arevt, buf, eacc = rest
+def degree_kernel(halves, pairs, each, last, deg_ref, *rest):
+    joined = [h * 2 * each for h in range(halves)]
+    count = 1 if last else halves
+    recvs, rest = rest[:count], rest[count:]
+    recvs = [(recvs[0], at) for at in joined] if last else [(ref, 0) for ref in recvs]
+    eins, rest = [(ref, 0) for ref in rest[:halves]], rest[halves:]
+    eprev, prow, pcol, ct, st, table = rest[:6]
+    count = halves if last else 1
+    outs, rest = rest[6 : 6 + count], rest[6 + count :]
+    outs = [(ref, 0) for ref in outs] if last else [(outs[0], at) for at in joined]
+    if not last:
+        eout, rest = rest[0], rest[1:]
+    a0, arev, a0t, arevt, buf, eacc = rest
     width = 2 * pairs + 1
-    devices = pairs // local
+    devices, part = recvs[0][0].shape[0], recvs[0][0].shape[2]
+    size = devices * part
     c = pl.program_id(0)
 
     @pl.when(c == 0)
@@ -225,15 +239,22 @@
         arevt[...] = onehot(pairs - 1 - r1, pcol[...])
         eacc[...] = eprev[...]
 
+    def gather(refs, at):
+        return jnp.concatenate(
+            [ref[:, base + at].astype(F32).reshape(size, 128) for ref, base in refs], 0
+        ).astype(BF16)
+
+    def scatter(refs, at, value):
+        for h, (ref, base) in enumerate(refs):
+            ref[:, base + at] = value[h * size : (h + 1) * size].reshape(devices, part, 128).astype(BF16)
+
     q = deg_ref[c]
-    at0 = pl.multiple_of(c * local, 16)
-    at1 = pl.multiple_of((each + c) * local, 16)
-    in0 = recv[:, pl.ds(at0, local), :].reshape(pairs, 128)
-    in1 = recv[:, pl.ds(at1, local), :].reshape(pairs, 128)
+    in0 = gather(recvs, c)
+    in1 = gather(recvs, each + c)
     u = dot(a0[...], jnp.concatenate([in0, in1], 1))
     v = dot(arev[...], in1)
     pick = onehot(jnp.broadcast_to(prow[...], (8, pairs)), q)
-    e = dot(pick, ein[...].reshape(pairs, 128))
+    e = dot(pick, gather(eins, 0))
     buf[0:pairs, :] = u[:, 128:]
     buf[pl.ds(q + 1, pairs), :] = u[:, :128]
     buf[pl.ds(q + 1 + pairs, pairs), :] = v
@@ -249,34 +270,35 @@
     f1 = jnp.where(row <= q, buf[0:pairs, :], 0.0).astype(BF16)
     back = jnp.where(row < pairs - 1 - q, buf[pl.ds(q + 1 + pairs, pairs), :], 0.0).astype(BF16)
     g = dot(a0t[...], jnp.concatenate([f0, f1], 1))
-    h = g[:, 128:] + dot(arevt[...], back)
-    out[:, pl.ds(at0, local), :] = g[:, :128].astype(BF16).reshape(devices, local, 128)
-    out[:, pl.ds(at1, local), :] = h.astype(BF16).reshape(devices, local, 128)
+    scatter(outs, c, g[:, :128])
+    scatter(outs, each + c, g[:, 128:] + dot(arevt[...], back))
     eacc[...] += jnp.where(pcol[...] == q, buf[width - 1 : width, :], 0.0)
 
     @pl.when(c == each - 1)
     def _():
         if last:
-            out[:, 2 * each * local :, :] = eacc[...].astype(BF16).reshape(devices, local, 128)
+            scatter(outs, 2 * each, eacc[...])
         else:
             eout[...] = eacc[...]
 
 
-def unpack_kernel(local, pairs, chunks, ord_ref, qrow_ref, cs_ref, *rest):
+def unpack_kernel(half, pairs, chunks, ord_ref, qrow_ref, cs_ref, *rest):
     backs = rest[:chunks]
-    out_ref, os, scr0, scr1, extra, q0, q1, sem = rest[chunks:]
+    out_ref, os3, scr0, scr1, extra, q0, q1, sem = rest[-8:]
+    part = cs_ref.shape[1]
     width = 2 * pairs + 1
-    devices = pairs // local
-    each = local // chunks
-    span = each * local
+    devices, each = backs[0].shape[0], backs[1].shape[1] // 2
+    span = each * part
+    os = os3.reshape((pairs + width) * part, 128)
     extra[...] = jnp.zeros(extra.shape, F32)
 
     def take(d, carry):
         for k, back in enumerate(backs):
-            at = pl.multiple_of(d * local * local + k * span, 16)
-            scr0[pl.ds(at, span), :] = back[d, 0:span, :].astype(F32)
-            scr1[pl.ds(at, span), :] = back[d, span : 2 * span, :].astype(F32)
-        extra[...] += backs[-1][d, 2 * span :, :].astype(F32)
+            at = pl.multiple_of((d * chunks + k) * span, 8)
+            base = half * 2 * each if k == 0 else 0
+            scr0[pl.ds(at, span), :] = back[d, base : base + each].astype(F32).reshape(span, 128)
+            scr1[pl.ds(at, span), :] = back[d, base + each : base + 2 * each].astype(F32).reshape(span, 128)
+        extra[...] += backs[-1][d, 2 * each].astype(F32)
         return carry
 
     lax.fori_loop(0, devices, take, 0)
@@ -287,22 +309,24 @@
     def step(r, carry):
         p = ord_ref[r]
         cl, sl, ch, sh = (cs_ref[i, pl.ds(r, 1), :] for i in range(4))
-        s0 = scr0[pl.ds(r, pairs, stride=local), :].astype(BF16)
-        s1 = scr1[pl.ds(r, pairs, stride=local), :].astype(BF16)
+        s0 = scr0[pl.ds(r, pairs, stride=part), :].astype(BF16)
+        s1 = scr1[pl.ds(r, pairs, stride=part), :].astype(BF16)
         both = dot(q0[...], jnp.concatenate([s0, s1], 1))
         low = dot(q1[...], s1)
 
         def put(pos, value):
-            os[pl.ds((pairs + pos) * local + r, pairs, stride=local), :] = value
+            os[pl.ds((pairs + pos) * part + r, pairs, stride=part), :] = value
 
         put(pairs + 1, rotate(both[:, 128:], ch, sh))
         put(-p, rotate(low, cl, sl))
         put(pairs - p, rotate(both[:, :128], cl, sl))
-        os[pl.ds((pairs + width - 1 - p) * local + r, 1), :] = rotate(extra[pl.ds(r, 1), :], ch, sh)
+        os[pl.ds((pairs + width - 1 - p) * part + r, 1), :] = rotate(extra[pl.ds(r, 1), :], ch, sh)
         return carry
 
-    lax.fori_loop(0, local, step, 0)
-    copy = pltpu.make_async_copy(os.at[pl.ds(pairs * local, width * local)], out_ref, sem)
+    lax.fori_loop(0, part, step, 0)
+    copy = pltpu.make_async_copy(
+        os3.at[pl.ds(pairs, width)], out_ref.at[:, pl.ds(half * part, part), :], sem
+    )
     copy.start()
     copy.wait()
 
@@ -323,92 +347,104 @@
     pairs = top // 2
     if local % 16 or channels != 128 or pairs % 128:
         return small_shards(coeffs_in, tables, order_pairs, degree_pairs, angles)
-    chunks = CHUNKS
-    each = local // chunks
+    chunks, halves = CHUNKS, HALVES
+    each, part = local // chunks, local // halves
     devices = lax.axis_size("deg")
     device = lax.axis_index("deg")
     my_orders = lax.dynamic_slice_in_dim(order_pairs, device * local, local)
     my_degrees = lax.dynamic_slice_in_dim(degree_pairs, device * local, local)
     params = pltpu.CompilerParams(vmem_limit_bytes=56 * 1024 * 1024)
+    cost = lambda flops, moved: pl.CostEstimate(flops=flops, bytes_accessed=moved, transcendentals=0)
     turn_in = jnp.stack(phases(my_orders, angles[2]) + phases(top - 1 - my_orders, angles[2]))
     turn_out = jnp.stack(phases(my_orders, angles[0]) + phases(top - 1 - my_orders, angles[0]))
+    standing = jnp.transpose(coeffs_in, (1, 0, 2))
+    rows = [2 * each + (k == 0) for k in range(chunks)]
+    back_rows = [2 * each + (k == chunks - 1) for k in range(chunks)]
+    square = pltpu.VMEM((pairs, pairs), BF16)
+    slots = pltpu.VMEM((pairs * part, 128), F32)
+    line = pltpu.VMEM((pairs + width, part, 128), F32)
+    scratch = [line, slots, slots, pltpu.VMEM((part, 128), F32), square, square, pltpu.SemaphoreType.DMA]
+    wire = lambda n: jax.ShapeDtypeStruct((devices, n, part, 128), BF16)
+    mine = [my_orders[h * part : (h + 1) * part] for h in range(halves)]
+    sends = [
+        pl.pallas_call(
+            functools.partial(pack_kernel, h, pairs, chunks),
+            name="pack",
+            out_shape=[wire(n) for n in rows],
+            in_specs=[SMEM, ANY, VMEM, VMEM],
+            out_specs=[VMEM] * chunks,
+            scratch_shapes=scratch,
+            compiler_params=params,
+            cost_estimate=cost(6 * 10**9 // halves, 13 * 10**6 // halves),
+        )(mine[h], standing, degree_pairs[:, None], turn_in[:, h * part : (h + 1) * part])
+        for h in range(halves)
+    ]
+    swap = functools.partial(lax.all_to_all, axis_name="deg", split_axis=0, concat_axis=0, tiled=True)
     ct, st = (
         jnp.pad(t, ((pairs, 7), (0, 0))) for t in phases(jnp.arange(width, dtype=jnp.int32), angles[1])
     )
-    flat = jnp.transpose(coeffs_in, (1, 0, 2)).reshape(width * local, channels)
-    main_rows = 2 * each * local
-    rows = [main_rows + (local if k == 0 else 0) for k in range(chunks)]
-    back_rows = [main_rows + (local if k == chunks - 1 else 0) for k in range(chunks)]
-    square = pltpu.VMEM((pairs, pairs), BF16)
-    slots = pltpu.VMEM((pairs * local, 128), F32)
-    line = pltpu.VMEM(((pairs + width) * local, 128), F32)
-    sends = pl.pallas_call(
-        functools.partial(pack_kernel, local, pairs, chunks),
-        name="pack",
-        out_shape=[jax.ShapeDtypeStruct((devices, n, 128), BF16) for n in rows],
-        in_specs=[SMEM, ANY, VMEM, VMEM],
-        out_specs=[VMEM] * chunks,
-        scratch_shapes=[line, slots, slots, pltpu.VMEM((local, 128), F32), square, square, pltpu.SemaphoreType.DMA],
-        compiler_params=params,
-        cost_estimate=pl.CostEstimate(flops=6 * 10**9, bytes_accessed=13 * 10**6, transcendentals=0),
-    )(my_orders, flat, degree_pairs[:, None], turn_in)
-    swap = functools.partial(lax.all_to_all, axis_name="deg", split_axis=0, concat_axis=0, tiled=True)
-    arrived = [swap(s) for s in sends]
-    extra_in = arrived[0][:, main_rows:, :]
+    by_part = jnp.transpose(order_pairs.reshape(devices, halves, part), (1, 0, 2)).reshape(-1)
+    prow, pcol = by_part[None, :], by_part[:, None]
+    tables = with_layout_constraint(tables, Layout((0, 1, 2)))
+    arrived = [[swap(sends[h][0]) for h in range(halves)]]
+    extra_in = [a[:, 2 * each :] for a in arrived[0]]
+    later = jnp.concatenate([sends[h][1] for h in range(halves)], 1)
+    later, tables, ct, st, pcol, extra_in = lax.optimization_barrier((later, tables, ct, st, pcol, extra_in))
+    arrived.append([swap(later)])
     extra_back = jnp.zeros((pairs, 128), F32)
     homes = []
     for k in range(chunks):
         last = k == chunks - 1
-        full2 = lambda c, deg: (0, 0)
-        full3 = lambda c, deg: (0, 0, 0)
-        out_shape = [jax.ShapeDtypeStruct((devices, back_rows[k], 128), BF16)]
-        out_specs = [pl.BlockSpec((devices, back_rows[k], 128), full3)]
+        full = lambda shape: pl.BlockSpec(shape, lambda c, deg: (0,) * len(shape))
+        out_shape = [wire(back_rows[k])] * halves if last else [wire(2 * each * halves)]
+        out_specs = [full(w.shape) for w in out_shape]
+        sent = len(out_shape)
         if not last:
-            out_shape.append(jax.ShapeDtypeStruct((pairs, 128), F32))
-            out_specs.append(pl.BlockSpec((pairs, 128), full2))
+            out_shape = out_shape + [jax.ShapeDtypeStruct((pairs, 128), F32)]
+            out_specs = out_specs + [full((pairs, 128))]
         done = pl.pallas_call(
-            functools.partial(degree_kernel, local, pairs, each, last),
+            functools.partial(degree_kernel, halves, pairs, each, last),
             name="degree",
             out_shape=out_shape,
             grid_spec=pltpu.PrefetchScalarGridSpec(
                 num_scalar_prefetch=1,
                 grid=(each,),
-                in_specs=[
-                    pl.BlockSpec((devices, rows[k], 128), full3),
-                    pl.BlockSpec((devices, local, 128), full3),
-                    pl.BlockSpec((pairs, 128), full2),
-                    pl.BlockSpec((1, pairs), full2),
-                    pl.BlockSpec((pairs, 1), full2),
-                    pl.BlockSpec(ct.shape, full2),
-                    pl.BlockSpec(st.shape, full2),
-                    pl.BlockSpec((None, width, width), lambda c, deg, k=k: (k * each + c, 0, 0)),
-                ],
+                in_specs=[full(a.shape) for a in arrived[k]]
+                + [full((devices, 1, part, 128))] * halves
+                + [full((pairs, 128)), full((1, pairs)), full((pairs, 1)), full(ct.shape), full(st.shape)]
+                + [pl.BlockSpec((None, width, width), lambda c, deg, k=k: (k * each + c, 0, 0))],
                 out_specs=out_specs,
                 scratch_shapes=[square] * 4
                 + [pltpu.VMEM((3 * pairs + 16, 128), F32), pltpu.VMEM((pairs, 128), F32)],
             ),
             compiler_params=params,
-            cost_estimate=pl.CostEstimate(
-                flops=16 * 10**9 // chunks, bytes_accessed=50 * 10**6 // chunks, transcendentals=0
-            ),
+            cost_estimate=cost(16 * 10**9 // chunks, 50 * 10**6 // chunks),
         )(
-            my_degrees[k * each : (k + 1) * each], arrived[k], extra_in, extra_back,
-            order_pairs[None, :], order_pairs[:, None], ct, st, tables,
+            my_degrees[k * each : (k + 1) * each], *arrived[k], *extra_in,
+            extra_back, prow, pcol, ct, st, tables,
         )
         if not last:
-            extra_back = done[1]
-        homes.append(swap(done[0]))
-    result = pl.pallas_call(
-        functools.partial(unpack_kernel, local, pairs, chunks),
-        name="unpack",
-        out_shape=jax.ShapeDtypeStruct((width * local, 128), F32),
-        in_specs=[SMEM, VMEM, VMEM] + [VMEM] * chunks,
-        out_specs=ANY,
-        scratch_shapes=[line, slots, slots, pltpu.VMEM((local, 128), F32), square, square, pltpu.SemaphoreType.DMA],
-        compiler_params=params,
-        cost_estimate=pl.CostEstimate(flops=6 * 10**9, bytes_accessed=13 * 10**6, transcendentals=0),
-    )(my_orders, degree_pairs[None, :], turn_out, *homes)
-    return jnp.transpose(result.reshape(width, local, 128), (1, 0, 2))
+            extra_back = done[sent]
+        homes.append([swap(d) for d in done[:sent]])
+    result = ()
+    for h in range(halves):
+        result = (
+            pl.pallas_call(
+                functools.partial(unpack_kernel, h, pairs, chunks),
+                name="unpack",
+                out_shape=jax.ShapeDtypeStruct((width, local, 128), F32),
+                in_specs=[SMEM, VMEM, VMEM] + [VMEM] * chunks + [ANY] * len(result),
+                out_specs=ANY,
+                scratch_shapes=scratch,
+                input_output_aliases={3 + chunks: 0} if result else {},
+                compiler_params=params,
+                cost_estimate=cost(6 * 10**9 // halves, 13 * 10**6 // halves),
+            )(
+                mine[h], degree_pairs[None, :], turn_out[:, h * part : (h + 1) * part],
+                homes[0][0], homes[1][h], *result,
+            ),
+        )
+    return jnp.transpose(result[0], (1, 0, 2))
 
 
 def solution(mesh):

time: 300 us -> 276 us (0.920)
  blocking collectives: 60.4 us -> 33.5 us
  starting transfers between devices: 13.3 us -> 23.4 us
  waiting for transfers between devices: 62.9 us -> 54.1 us
  Pallas kernels: 120 us -> 115 us
  local copies, waits for them, and re-layouts: 37.7 us -> 40.8 us
    all_to_all x1, blocking collectives: 60.4 us -> 33.5 us  [shards(): homes.append([swap(d) for d in done[:sent]])]
    all_to_all x3 -> x5, starting transfers between devices: 13.3 us -> 23.4 us  [the longest x2 10.9 us: shards(): arrived = [[swap(sends[h][0]) for h in range(halves)]]]
    all_to_all x3 -> x5, waiting for transfers between devices: 62.9 us -> 54.1 us  [the longest x2 27.9 us: shards(): homes.append([swap(d) for d in done[:sent]])]
    pallas_call x4 -> x6, Pallas kernels: 120 us -> 115 us  [the longest x2 74 us: shards(): pl.pallas_call(functools.partial(degree_kernel, halves, pairs, each, last...]
    unnamed x11 -> x15, local copies, waits for them, and re-layouts: 28.8 us -> 28.4 us
  transfers between devices with their start and end apart: 3 -> 5, of which waited for: 2 -> 4; matrix products, arithmetic and copies ran while one was open for 11% -> 13% of each run, Pallas kernels for 25% -> 34%
where the time goes in v2:
time: 276 us; the launch traced here: 275 us
  Pallas kernels  115 us (42%)
  waiting for transfers between devices  54.1 us (20%)
  local copies, waits for them, and re-layouts  40.8 us (15%)
  blocking collectives  33.5 us (12%)
  starting transfers between devices  23.4 us (8%)
  other arithmetic  7.22 us (3%)
    pallas_call x2, Pallas kernels, shards(): pl.pallas_call(functools.partial(degree_kernel, halves, pairs, each, last...  74 us
    all_to_all x1, blocking collectives, shards(): homes.append([swap(d) for d in done[:sent]])  33.5 us
    unnamed x15, local copies, waits for them, and re-layouts  28.4 us
    all_to_all x2, waiting for transfers between devices, shards(): homes.append([swap(d) for d in done[:sent]])  27.9 us
    pallas_call x2, Pallas kernels, shards(): pl.pallas_call(functools.partial(unpack_kernel, h, pairs, chunks), name='...  21.9 us
    pallas_call x2, Pallas kernels, shards(): pl.pallas_call(functools.partial(pack_kernel, h, pairs, chunks), name='pa...  19.5 us
    all_to_all x2, waiting for transfers between devices, shards(): arrived = [[swap(sends[h][0]) for h in range(halves)]]  17.9 us
    all_to_all x2, starting transfers between devices, shards(): arrived = [[swap(sends[h][0]) for h in range(halves)]]  10.9 us
  transfers between devices with their start and end apart: 5, of which 4 were waited for; matrix products, arithmetic and copies ran while one was open for 13% of the time, Pallas kernels for 34%

profile of v2, /device:TPU:0, one launch (start us, length us, event | category | flops | bytes accessed | tf_op | source)
XLA Modules:
  0.0 274.6 jit_solution(3151306854130497080)
XLA Ops:
  0.0 1.4 fusion.22
  1.4 1.3 fusion.6
  2.8 0.7 fusion.23
  3.4 1.3 fusion.11
  4.7 0.1 broadcast_select_fusion.2
  4.8 0.1 stack_broadcast_in_dim.10
  4.9 0.1 stack_broadcast_in_dim.9
  4.9 0.1 stack_broadcast_in_dim.8
  5.0 0.1 stack_broadcast_in_dim.11
  5.1 0.6 fusion.20
  5.7 1.5 copy.8.qcol_ref
  7.2 9.8 %pack.3 = (bf16[32,17,8,128]{3,2,1,0:T(8,128)(2,1)}, bf16[32,16,8,128]{3,2,1,0:T(8,128)(2,1)}) custom-call(s32[8]{0:T(128)} %get-tuple-element.68.ord_ref, f32[1025,16,128]{2,1,0:T(8,128)} %bitcast.12, s32[512,1]{1,0:T(8,128)} %copy.8.qcol_ref, f32[4,8,128]{2,1,0:T(8,128)} %get-tuple-element.47.cs_ref), custom_call_target="tpu_custom_call" | custom-call | flops 3000000000 | bytes 6500000 | tf_op jit(solution)/shard_map/pack/pallas_call | solution.py:370
  17.0 7.3 %all-to-all-start.1 = ((bf16[32,17,8,128]{3,2,1,0:T(8,128)(2,1)}), bf16[32,17,8,128]{3,2,1,0:T(8,128)(2,1)S(1)}, u32[]{:S(2)}, u32[]{:S(2)}) async-start(bf16[32,17,8,128]{3,2,1,0:T(8,128)(2,1)} %get-tuple-element.21), calls=%async_computation.1 | async-start | bytes 2228224 | tf_op jit(solution)/shard_map/all_to_all | solution.py:389
  24.3 9.8 %pack.2 = (bf16[32,17,8,128]{3,2,1,0:T(8,128)(2,1)}, bf16[32,16,8,128]{3,2,1,0:T(8,128)(2,1)}) custom-call(s32[8]{0:T(128)} %get-tuple-element.67.ord_ref, f32[1025,16,128]{2,1,0:T(8,128)} %bitcast.13, s32[512,1]{1,0:T(8,128)} %copy.8.qcol_ref, f32[4,8,128]{2,1,0:T(8,128)} %get-tuple-element.48.cs_ref), custom_call_target="tpu_custom_call" | custom-call | flops 3000000000 | bytes 6500000 | tf_op jit(solution)/shard_map/pack/pallas_call | solution.py:370
  34.1 0.0 copy-start.6
  34.1 17.9 %all-to-all-done.1.rest_1_ = bf16[32,17,8,128]{3,2,1,0:T(8,128)(2,1)S(1)} async-done(((bf16[32,17,8,128]{3,2,1,0:T(8,128)(2,1)}), bf16[32,17,8,128]{3,2,1,0:T(8,128)(2,1)S(1)}, u32[]{:S(2)}, u32[]{:S(2)}) %all-to-all-start.1) | async-done | bytes 1114144 | tf_op jit(solution)/shard_map/all_to_all | solution.py:389
  52.0 3.6 %all-to-all-start = ((bf16[32,17,8,128]{3,2,1,0:T(8,128)(2,1)}), bf16[32,17,8,128]{3,2,1,0:T(8,128)(2,1)S(1)}, u32[]{:S(2)}, u32[]{:S(2)}) async-start(bf16[32,17,8,128]{3,2,1,0:T(8,128)(2,1)} %get-tuple-element.20), calls=%async_computation | async-start | bytes 2228224 | tf_op jit(solution)/shard_map/all_to_all | solution.py:389
  55.6 0.1 reshape.264
  55.7 0.1 broadcast_in_dim_reshape.6
  55.8 0.7 fusion
  56.6 0.7 fusion.2
  57.3 0.3 broadcast_select_fusion
  57.6 1.0 pad.11.rest_8_.rest_7_
  58.6 26.0 %copy.10.rest_9_.rest_8_ = bf16[16,1025,1025]{2,1,0:T(8,128)(2,1)} copy(bf16[16,1025,1025]{2,0,1:T(8,128)(2,1)} %param.6) | data formatting | bytes 67240000 | tf_op args[1]
  84.7 2.7 pad_maximum_fusion
  87.4 0.6 slice.58.rest_3_.rest_2_
  88.0 0.0 all-to-all-done.rest_0_
  88.0 0.7 slice.57.rest_2_.rest_1_
  88.7 1.2 pad.10.rest_7_.rest_6_
  89.9 5.8 %all-to-all-start.3 = ((bf16[32,32,8,128]{3,2,1,0:T(8,128)(2,1)}), bf16[32,32,8,128]{3,2,1,0:T(8,128)(2,1)S(1)}, u32[]{:S(2)}, u32[]{:S(2)}) async-start(bf16[32,32,8,128]{3,2,1,0:T(8,128)(2,1)} %pad_maximum_fusion), calls=%async_computation.3 | async-start | bytes 4194304 | tf_op jit(solution)/shard_map/all_to_all | solution.py:393
  95.7 0.8 dynamic_slice.7
  96.5 0.7 broadcast_in_dim_reshape.7.rest_5_.rest_4_
  97.2 0.6 fusion.21
  97.8 0.8 copy.13.rest_6_.rest_5_
  98.6 0.7 broadcast_in_dim.141.rest_4_
  99.4 37.0 %degree.2 = (bf16[32,32,8,128]{3,2,1,0:T(8,128)(2,1)}, f32[512,128]{1,0:T(8,128)}) custom-call(s32[8]{0:T(128)} %get-tuple-element.50.deg_ref, bf16[32,17,8,128]{3,2,1,0:T(8,128)(2,1)} %copy-done.3, bf16[32,17,8,128]{3,2,1,0:T(8,128)(2,1)} %copy-done.2, bf16[32,1,8,128]{3,2,1,0:T(8,128)(2,1)} %slice.57.rest_2_.rest_1_, ...), custom_call_target="tpu_custom_call" | custom-call | flops 8000000000 | bytes 25000000 | tf_op jit(solution)/shard_map/degree/pallas_call | solution.py:405
  136.3 8.3 %all-to-all-done.3.rest_0_ = bf16[32,32,8,128]{3,2,1,0:T(8,128)(2,1)S(1)} async-done(((bf16[32,32,8,128]{3,2,1,0:T(8,128)(2,1)}), bf16[32,32,8,128]{3,2,1,0:T(8,128)(2,1)S(1)}, u32[]{:S(2)}, u32[]{:S(2)}) %all-to-all-start.3) | async-done | bytes 2097184 | tf_op jit(solution)/shard_map/all_to_all | solution.py:393
  144.6 1.3 copy-done.1
  146.0 4.0 %all-to-all-start.2 = ((bf16[32,32,8,128]{3,2,1,0:T(8,128)(2,1)}), bf16[32,32,8,128]{3,2,1,0:T(8,128)(2,1)S(1)}, u32[]{:S(2)}, u32[]{:S(2)}) async-start(bf16[32,32,8,128]{3,2,1,0:T(8,128)(2,1)} %get-tuple-element.30), calls=%async_computation.2 | async-start | bytes 4194304 | tf_op jit(solution)/shard_map/all_to_all | solution.py:428
  150.0 37.0 %degree.3 = (bf16[32,17,8,128]{3,2,1,0:T(8,128)(2,1)}, bf16[32,17,8,128]{3,2,1,0:T(8,128)(2,1)}) custom-call(s32[8]{0:T(128)} %get-tuple-element.49.deg_ref, bf16[32,32,8,128]{3,2,1,0:T(8,128)(2,1)} %copy-done.1, bf16[32,1,8,128]{3,2,1,0:T(8,128)(2,1)} %slice.57.rest_2_.rest_1_, bf16[32,1,8,128]{3,2,1,0:T(8,128)(2,1)} %slice.58.rest_3_.rest_2_, ...), custom_call_target="tpu_custom_call" | custom-call | flops 8000000000 | bytes 25000000 | tf_op jit(solution)/shard_map/degree/pallas_call | solution.py:405
  187.0 11.9 %all-to-all-done.2.rest_0_ = bf16[32,32,8,128]{3,2,1,0:T(8,128)(2,1)S(1)} async-done(((bf16[32,32,8,128]{3,2,1,0:T(8,128)(2,1)}), bf16[32,32,8,128]{3,2,1,0:T(8,128)(2,1)S(1)}, u32[]{:S(2)}, u32[]{:S(2)}) %all-to-all-start.2) | async-done | bytes 2097184 | tf_op jit(solution)/shard_map/all_to_all | solution.py:428
  198.9 33.5 %all_to_all.30.rest_1_ = bf16[32,17,8,128]{3,2,1,0:T(8,128)(2,1)} all-to-all(bf16[32,17,8,128]{3,2,1,0:T(8,128)(2,1)} %get-tuple-element.34), channel_id=1, replica_groups=mesh['grp'=1,'deg'=32] {'deg'}, dimensions={0} | all-to-all | bytes 2228224 | tf_op jit(solution)/shard_map/all_to_all | solution.py:428
  232.4 2.7 all-to-all-start.4
  235.0 0.6 fusion.19
  235.6 10.9 %unpack.2.rest_2_ = f32[1025,16,128]{2,1,0:T(8,128)} custom-call(s32[8]{0:T(128)} %get-tuple-element.67.ord_ref, s32[1,512]{1,0:T(1,128)} %bitcast.10, f32[4,8,128]{2,1,0:T(8,128)} %get-tuple-element.45.cs_ref, bf16[32,32,8,128]{3,2,1,0:T(8,128)(2,1)} %copy-done, bf16[32,17,8,128]{3,2,1,0:T(8,128)(2,1)} %all_to_all.30.rest_1_), custom_call_target="tpu_custom_call" | custom-call | flops 3000000000 | bytes 6500000 | tf_op jit(solution)/shard_map/unpack/pallas_call | solution.py:432
  246.6 16.0 %all-to-all-done.4.rest_1_ = bf16[32,17,8,128]{3,2,1,0:T(8,128)(2,1)S(1)} async-done(((bf16[32,17,8,128]{3,2,1,0:T(8,128)(2,1)}), bf16[32,17,8,128]{3,2,1,0:T(8,128)(2,1)S(1)}, u32[]{:S(2)}, u32[]{:S(2)}) %all-to-all-start.4) | async-done | bytes 1114144 | tf_op jit(solution)/shard_map/all_to_all | solution.py:428
  262.6 1.0 copy-done.4
  263.7 10.9 %unpack.3 = f32[1025,16,128]{2,1,0:T(8,128)} custom-call(s32[8]{0:T(128)} %get-tuple-element.68.ord_ref, s32[1,512]{1,0:T(1,128)} %bitcast.11, f32[4,8,128]{2,1,0:T(8,128)} %get-tuple-element.46.cs_ref, bf16[32,32,8,128]{3,2,1,0:T(8,128)(2,1)} %copy-done, bf16[32,17,8,128]{3,2,1,0:T(8,128)(2,1)} %copy-done.4, ...), custom_call_target="tpu_custom_call", output_to_operand_aliasing={{}: (5, {})} | custom-call | flops 3000000000 | bytes 6500000 | tf_op jit(solution)/shard_map/unpack/pallas_call | solution.py:432
  (15 shorter events, 0.0 us)
Async XLA Ops:
  17.0 35.0 %all-to-all-start.1 = ((bf16[32,17,8,128]{3,2,1,0:T(8,128)(2,1)}), bf16[32,17,8,128]{3,2,1,0:T(8,128)(2,1)S(1)}, u32[]{:S(2)}, u32[]{:S(2)}) async-start(bf16[32,17,8,128]{3,2,1,0:T(8,128)(2,1)} %get-tuple-element.21), calls=%async_computation.1 | async-start | bytes 2228224 | tf_op jit(solution)/shard_map/all_to_all | solution.py:389
  34.1 21.5 %copy-start.6 = (s32[512]{0:T(512)S(1)}, s32[512]{0:T(512)}, u32[]{:S(2)}) copy-start(s32[512]{0:T(512)} %param.7) | copy-start | bytes 6148
  52.0 35.4 %copy-start.2 = (bf16[32,17,8,128]{3,2,1,0:T(8,128)(2,1)}, bf16[32,17,8,128]{3,2,1,0:T(8,128)(2,1)S(1)}, u32[]{:S(2)}) copy-start(bf16[32,17,8,128]{3,2,1,0:T(8,128)(2,1)S(1)} %all-to-all-done.1.rest_1_) | copy-start | bytes 3342340
  52.0 36.1 %all-to-all-start = ((bf16[32,17,8,128]{3,2,1,0:T(8,128)(2,1)}), bf16[32,17,8,128]{3,2,1,0:T(8,128)(2,1)S(1)}, u32[]{:S(2)}, u32[]{:S(2)}) async-start(bf16[32,17,8,128]{3,2,1,0:T(8,128)(2,1)} %get-tuple-element.20), calls=%async_computation | async-start | bytes 2228224 | tf_op jit(solution)/shard_map/all_to_all | solution.py:389
  58.6 26.0 %copy-start.5 = (bf16[32,16,8,128]{3,2,1,0:T(8,128)(2,1)S(1)}, bf16[32,16,8,128]{3,2,1,0:T(8,128)(2,1)}, u32[]{:S(2)}) copy-start(bf16[32,16,8,128]{3,2,1,0:T(8,128)(2,1)} %get-tuple-element.23) | copy-start | bytes 3145732
  88.0 1.9 copy-start.3
  89.9 54.7 %all-to-all-start.3 = ((bf16[32,32,8,128]{3,2,1,0:T(8,128)(2,1)}), bf16[32,32,8,128]{3,2,1,0:T(8,128)(2,1)S(1)}, u32[]{:S(2)}, u32[]{:S(2)}) async-start(bf16[32,32,8,128]{3,2,1,0:T(8,128)(2,1)} %pad_maximum_fusion), calls=%async_computation.3 | async-start | bytes 4194304 | tf_op jit(solution)/shard_map/all_to_all | solution.py:393
  144.6 1.3 copy-start.1
  146.0 52.9 %all-to-all-start.2 = ((bf16[32,32,8,128]{3,2,1,0:T(8,128)(2,1)}), bf16[32,32,8,128]{3,2,1,0:T(8,128)(2,1)S(1)}, u32[]{:S(2)}, u32[]{:S(2)}) async-start(bf16[32,32,8,128]{3,2,1,0:T(8,128)(2,1)} %get-tuple-element.30), calls=%async_computation.2 | async-start | bytes 4194304 | tf_op jit(solution)/shard_map/all_to_all | solution.py:428
  198.9 33.5 %copy-start = (bf16[32,32,8,128]{3,2,1,0:T(8,128)(2,1)}, bf16[32,32,8,128]{3,2,1,0:T(8,128)(2,1)S(1)}, u32[]{:S(2)}) copy-start(bf16[32,32,8,128]{3,2,1,0:T(8,128)(2,1)S(1)} %all-to-all-done.2.rest_0_) | copy-start | bytes 6291460
  232.4 30.3 %all-to-all-start.4 = ((bf16[32,17,8,128]{3,2,1,0:T(8,128)(2,1)}), bf16[32,17,8,128]{3,2,1,0:T(8,128)(2,1)S(1)}, u32[]{:S(2)}, u32[]{:S(2)}) async-start(bf16[32,17,8,128]{3,2,1,0:T(8,128)(2,1)} %get-tuple-element.33), calls=%async_computation.4 | async-start | bytes 2228224 | tf_op jit(solution)/shard_map/all_to_all | solution.py:428
  262.6 1.0 copy-start.4

commit v3 on v2

--- a/solution.py
+++ b/solution.py
@@ -164,10 +164,26 @@
     return lax.broadcasted_iota(jnp.int32, shape, dim)
 
 
-def pack_kernel(half, pairs, chunks, ord_ref, x_ref, qcol_ref, cs_ref, *rest):
+def turning(orders, angle, top):
+    rows = len(orders)
+    shape = (rows, 128)
+    low = jnp.zeros(shape, jnp.int32)
+    for r, order in enumerate(orders):
+        low = jnp.where(iota(shape, 0) == r, order, low)
+    first = iota(shape, 1) < 64
+    out = []
+    for order in (low, top - 1 - low):
+        turn = order.astype(F32) * angle
+        sine = jnp.sin(turn)
+        out += [jnp.cos(turn), jnp.where(first, sine, -sine)]
+    return out
+
+
+def pack_kernel(half, local, pairs, chunks, ord_ref, angle_ref, x_ref, qrow_ref, *rest):
     outs = rest[:chunks]
-    xs3, scr0, scr1, extra, q0, q1, sem = rest[chunks:]
-    part = cs_ref.shape[1]
+    xs3, scr0, scr1, extra, cs_ref, q0, q1, sem = rest[chunks:]
+    part = xs3.shape[1]
+    start = lax.axis_index("deg") * local + half * part
     width = 2 * pairs + 1
     devices, each = outs[0].shape[0], outs[1].shape[1] // 2
     copy = pltpu.make_async_copy(
@@ -175,14 +191,16 @@
     )
     copy.start()
     xs = xs3.reshape((pairs + width) * part, 128)
-    column = iota((pairs, pairs), 1)
-    q0[...] = onehot(column, pairs - 1 - qcol_ref[...])
-    q1[...] = onehot(column, qcol_ref[...])
+    level = iota((pairs, pairs), 0)
+    q0[...] = jnp.where(pairs - 1 - level == qrow_ref[...], 1.0, 0.0).T.astype(BF16)
+    q1[...] = jnp.where(level == qrow_ref[...], 1.0, 0.0).T.astype(BF16)
+    for i, t in enumerate(turning([ord_ref[start + r] for r in range(part)], angle_ref[2], width - 1)):
+        cs_ref[i] = t
     copy.wait()
     row = iota((pairs, 1), 0)
 
-    def step(r, carry):
-        p = ord_ref[r]
+    def one(r):
+        p = ord_ref[start + r]
         cl, sl, ch, sh = (cs_ref[i, pl.ds(r, 1), :] for i in range(4))
 
         def load(pos):
@@ -192,12 +210,20 @@
         mid = rotate(load(pairs - p), cl, sl).astype(BF16)
         high = jnp.where(row >= pairs - p, rotate(load(pairs + 1), ch, sh), 0.0).astype(BF16)
         both = dot(q0[...], jnp.concatenate([mid, high], 1))
-        scr0[pl.ds(r, pairs, stride=part), :] = both[:, :128]
-        scr1[pl.ds(r, pairs, stride=part), :] = both[:, 128:] + dot(q1[...], low)
         extra[pl.ds(r, 1), :] = rotate(xs[pl.ds((pairs + width - 1 - p) * part + r, 1), :], ch, sh)
+        return low, both
+
+    def step(i, carry):
+        r = 2 * i
+        low_a, both_a = one(r)
+        low_b, both_b = one(r + 1)
+        lows = dot(q1[...], jnp.concatenate([low_a, low_b], 1))
+        for at, both, low in ((r, both_a, lows[:, :128]), (r + 1, both_b, lows[:, 128:])):
+            scr0[pl.ds(at, pairs, stride=part), :] = both[:, :128]
+            scr1[pl.ds(at, pairs, stride=part), :] = both[:, 128:] + low
         return carry
 
-    lax.fori_loop(0, part, step, 0)
+    lax.fori_loop(0, part // 2, step, 0)
     span = each * part
 
     def emit(d, carry):
@@ -282,10 +308,11 @@
             eout[...] = eacc[...]
 
 
-def unpack_kernel(half, pairs, chunks, ord_ref, qrow_ref, cs_ref, *rest):
+def unpack_kernel(half, local, pairs, chunks, ord_ref, angle_ref, qrow_ref, *rest):
     backs = rest[:chunks]
-    out_ref, os3, scr0, scr1, extra, q0, q1, sem = rest[-8:]
-    part = cs_ref.shape[1]
+    out_ref, os3, scr0, scr1, extra, cs_ref, q0, q1, sem = rest[-9:]
+    part = os3.shape[1]
+    start = lax.axis_index("deg") * local + half * part
     width = 2 * pairs + 1
     devices, each = backs[0].shape[0], backs[1].shape[1] // 2
     span = each * part
@@ -305,25 +332,32 @@
     row = iota((pairs, pairs), 0)
     q0[...] = onehot(pairs - 1 - row, qrow_ref[...])
     q1[...] = onehot(row, qrow_ref[...])
-
-    def step(r, carry):
-        p = ord_ref[r]
-        cl, sl, ch, sh = (cs_ref[i, pl.ds(r, 1), :] for i in range(4))
-        s0 = scr0[pl.ds(r, pairs, stride=part), :].astype(BF16)
-        s1 = scr1[pl.ds(r, pairs, stride=part), :].astype(BF16)
-        both = dot(q0[...], jnp.concatenate([s0, s1], 1))
-        low = dot(q1[...], s1)
-
-        def put(pos, value):
-            os[pl.ds((pairs + pos) * part + r, pairs, stride=part), :] = value
-
-        put(pairs + 1, rotate(both[:, 128:], ch, sh))
-        put(-p, rotate(low, cl, sl))
-        put(pairs - p, rotate(both[:, :128], cl, sl))
-        os[pl.ds((pairs + width - 1 - p) * part + r, 1), :] = rotate(extra[pl.ds(r, 1), :], ch, sh)
+    for i, t in enumerate(turning([ord_ref[start + r] for r in range(part)], angle_ref[0], width - 1)):
+        cs_ref[i] = t
+
+    def step(i, carry):
+        r = 2 * i
+        s1s, boths = [], []
+        for at in (r, r + 1):
+            s0 = scr0[pl.ds(at, pairs, stride=part), :].astype(BF16)
+            s1 = scr1[pl.ds(at, pairs, stride=part), :].astype(BF16)
+            s1s.append(s1)
+            boths.append(dot(q0[...], jnp.concatenate([s0, s1], 1)))
+        lows = dot(q1[...], jnp.concatenate(s1s, 1))
+        for at, both, low in ((r, boths[0], lows[:, :128]), (r + 1, boths[1], lows[:, 128:])):
+            p = ord_ref[start + at]
+            cl, sl, ch, sh = (cs_ref[i, pl.ds(at, 1), :] for i in range(4))
+
+            def put(pos, value):
+                os[pl.ds((pairs + pos) * part + at, pairs, stride=part), :] = value
+
+            put(pairs + 1, rotate(both[:, 128:], ch, sh))
+            put(-p, rotate(low, cl, sl))
+            put(pairs - p, rotate(both[:, :128], cl, sl))
+            os[pl.ds((pairs + width - 1 - p) * part + at, 1), :] = rotate(extra[pl.ds(at, 1), :], ch, sh)
         return carry
 
-    lax.fori_loop(0, part, step, 0)
+    lax.fori_loop(0, part // 2, step, 0)
     copy = pltpu.make_async_copy(
         os3.at[pl.ds(pairs, width)], out_ref.at[:, pl.ds(half * part, part), :], sem
     )
@@ -351,32 +385,28 @@
     each, part = local // chunks, local // halves
     devices = lax.axis_size("deg")
     device = lax.axis_index("deg")
-    my_orders = lax.dynamic_slice_in_dim(order_pairs, device * local, local)
     my_degrees = lax.dynamic_slice_in_dim(degree_pairs, device * local, local)
     params = pltpu.CompilerParams(vmem_limit_bytes=56 * 1024 * 1024)
     cost = lambda flops, moved: pl.CostEstimate(flops=flops, bytes_accessed=moved, transcendentals=0)
-    turn_in = jnp.stack(phases(my_orders, angles[2]) + phases(top - 1 - my_orders, angles[2]))
-    turn_out = jnp.stack(phases(my_orders, angles[0]) + phases(top - 1 - my_orders, angles[0]))
     standing = jnp.transpose(coeffs_in, (1, 0, 2))
     rows = [2 * each + (k == 0) for k in range(chunks)]
     back_rows = [2 * each + (k == chunks - 1) for k in range(chunks)]
     square = pltpu.VMEM((pairs, pairs), BF16)
     slots = pltpu.VMEM((pairs * part, 128), F32)
     line = pltpu.VMEM((pairs + width, part, 128), F32)
-    scratch = [line, slots, slots, pltpu.VMEM((part, 128), F32), square, square, pltpu.SemaphoreType.DMA]
+    scratch = [line, slots, slots, pltpu.VMEM((part, 128), F32), pltpu.VMEM((4, part, 128), F32), square, square, pltpu.SemaphoreType.DMA]
     wire = lambda n: jax.ShapeDtypeStruct((devices, n, part, 128), BF16)
-    mine = [my_orders[h * part : (h + 1) * part] for h in range(halves)]
     sends = [
         pl.pallas_call(
-            functools.partial(pack_kernel, h, pairs, chunks),
+            functools.partial(pack_kernel, h, local, pairs, chunks),
             name="pack",
             out_shape=[wire(n) for n in rows],
-            in_specs=[SMEM, ANY, VMEM, VMEM],
+            in_specs=[SMEM, SMEM, ANY, VMEM],
             out_specs=[VMEM] * chunks,
             scratch_shapes=scratch,
             compiler_params=params,
             cost_estimate=cost(6 * 10**9 // halves, 13 * 10**6 // halves),
-        )(mine[h], standing, degree_pairs[:, None], turn_in[:, h * part : (h + 1) * part])
+        )(order_pairs, angles, standing, degree_pairs[None, :])
         for h in range(halves)
     ]
     swap = functools.partial(lax.all_to_all, axis_name="deg", split_axis=0, concat_axis=0, tiled=True)
@@ -385,11 +415,15 @@
     )
     by_part = jnp.transpose(order_pairs.reshape(devices, halves, part), (1, 0, 2)).reshape(-1)
     prow, pcol = by_part[None, :], by_part[:, None]
-    tables = with_layout_constraint(tables, Layout((0, 1, 2)))
-    arrived = [[swap(sends[h][0]) for h in range(halves)]]
+    tabled = [
+        with_layout_constraint(tables[k * each : (k + 1) * each], Layout((0, 1, 2))) for k in range(chunks)
+    ]
+    arrived = [[swap(sends[0][0])]]
+    early, tabled[0], ct, st, prow, pcol = lax.optimization_barrier((sends[1][0], tabled[0], ct, st, prow, pcol))
+    arrived[0].append(swap(early))
     extra_in = [a[:, 2 * each :] for a in arrived[0]]
     later = jnp.concatenate([sends[h][1] for h in range(halves)], 1)
-    later, tables, ct, st, pcol, extra_in = lax.optimization_barrier((later, tables, ct, st, pcol, extra_in))
+    later, tabled[1], extra_in = lax.optimization_barrier((later, tabled[1], extra_in))
     arrived.append([swap(later)])
     extra_back = jnp.zeros((pairs, 128), F32)
     homes = []
@@ -412,7 +446,7 @@
                 in_specs=[full(a.shape) for a in arrived[k]]
                 + [full((devices, 1, part, 128))] * halves
                 + [full((pairs, 128)), full((1, pairs)), full((pairs, 1)), full(ct.shape), full(st.shape)]
-                + [pl.BlockSpec((None, width, width), lambda c, deg, k=k: (k * each + c, 0, 0))],
+                + [pl.BlockSpec((None, width, width), lambda c, deg: (c, 0, 0))],
                 out_specs=out_specs,
                 scratch_shapes=[square] * 4
                 + [pltpu.VMEM((3 * pairs + 16, 128), F32), pltpu.VMEM((pairs, 128), F32)],
@@ -421,7 +455,7 @@
             cost_estimate=cost(16 * 10**9 // chunks, 50 * 10**6 // chunks),
         )(
             my_degrees[k * each : (k + 1) * each], *arrived[k], *extra_in,
-            extra_back, prow, pcol, ct, st, tables,
+            extra_back, prow, pcol, ct, st, tabled[k],
         )
         if not last:
             extra_back = done[sent]
@@ -430,18 +464,17 @@
     for h in range(halves):
         result = (
             pl.pallas_call(
-                functools.partial(unpack_kernel, h, pairs, chunks),
+                functools.partial(unpack_kernel, h, local, pairs, chunks),
                 name="unpack",
                 out_shape=jax.ShapeDtypeStruct((width, local, 128), F32),
-                in_specs=[SMEM, VMEM, VMEM] + [VMEM] * chunks + [ANY] * len(result),
+                in_specs=[SMEM, SMEM, VMEM] + [VMEM] * chunks + [ANY] * len(result),
                 out_specs=ANY,
                 scratch_shapes=scratch,
                 input_output_aliases={3 + chunks: 0} if result else {},
                 compiler_params=params,
                 cost_estimate=cost(6 * 10**9 // halves, 13 * 10**6 // halves),
             )(
-                mine[h], degree_pairs[None, :], turn_out[:, h * part : (h + 1) * part],
-                homes[0][0], homes[1][h], *result,
+                order_pairs, angles, degree_pairs[None, :], homes[0][0], homes[1][h], *result,
             ),
         )
     return jnp.transpose(result[0], (1, 0, 2))

time: 276 us -> 288 us (1.043)
  local copies, waits for them, and re-layouts: 40.8 us -> 71.8 us
  waiting for transfers between devices: 54.1 us -> 45.5 us
  Pallas kernels: 115 us -> 109 us
  other arithmetic: 7.22 us -> 3.16 us
    optimization_barrier x1 -> x3, local copies, waits for them, and re-layouts: 0.85 us -> 37.6 us  [the longest x2 19.1 us: shards(): lax.optimization_barrier((sends[1][0], tabled[0], ct, st, prow, pcol))]
    unnamed x15 -> x18, local copies, waits for them, and re-layouts: 28.4 us -> 2.7 us
    slice x3 -> x1, local copies, waits for them, and re-layouts: 1.9 us -> 24.6 us  [shards(): tables[k * each:(k + 1) * each]]
    all_to_all x2, waiting for transfers between devices: 17.9 us -> 7.06 us  [the longest x1 7.06 us: shards(): arrived[0].append(swap(early))]
    pallas_call x4, Pallas kernels: 41.4 us -> 35.3 us  [the longest x2 19.5 us: shards(): pl.pallas_call(functools.partial(unpack_kernel, h, local, pairs, chunks),...]
  transfers between devices with their start and end apart: 5 -> 5, of which waited for: 4 -> 4; matrix products, arithmetic and copies ran while one was open for 13% -> 25% of each run, Pallas kernels for 34% -> 32%
where the time goes in v3:
time: 288 us; the launch traced here: 287 us
  Pallas kernels  109 us (38%)
  local copies, waits for them, and re-layouts  71.8 us (25%)
  waiting for transfers between devices  45.5 us (16%)
  blocking collectives  33.5 us (12%)
  starting transfers between devices  23.6 us (8%)
  other arithmetic  3.16 us (1%)
    pallas_call x2, Pallas kernels, shards(): pl.pallas_call(functools.partial(degree_kernel, halves, pairs, each, last...  74 us
    all_to_all x1, blocking collectives, shards(): homes.append([swap(d) for d in done[:sent]])  33.5 us
    all_to_all x2, waiting for transfers between devices, shards(): homes.append([swap(d) for d in done[:sent]])  29.5 us
    slice x1, local copies, waits for them, and re-layouts, shards(): tables[k * each:(k + 1) * each]  24.6 us
    pallas_call x2, Pallas kernels, shards(): pl.pallas_call(functools.partial(unpack_kernel, h, local, pairs, chunks),...  19.5 us
    optimization_barrier x2, local copies, waits for them, and re-layouts, shards(): lax.optimization_barrier((sends[1][0], tabled[0], ct, st, prow, pcol))  19.1 us
    optimization_barrier x1, local copies, waits for them, and re-layouts, shards(): lax.optimization_barrier((later, tabled[1], extra_in))  18.4 us
    pallas_call x2, Pallas kernels, shards(): pl.pallas_call(functools.partial(pack_kernel, h, local, pairs, chunks), n...  15.8 us
  transfers between devices with their start and end apart: 5, of which 4 were waited for; matrix products, arithmetic and copies ran while one was open for 25% of the time, Pallas kernels for 32%

profile of v3, /device:TPU:0, one launch (start us, length us, event | category | flops | bytes accessed | tf_op | source)
XLA Modules:
  0.0 287.3 jit_solution(14612021459690068500)
XLA Ops:
  0.0 7.9 %pack.2 = (bf16[32,17,8,128]{3,2,1,0:T(8,128)(2,1)}, bf16[32,16,8,128]{3,2,1,0:T(8,128)(2,1)}) custom-call(s32[512]{0:T(512)} %ord_ref.7, f32[3]{0:T(128)} %angle_ref.7, f32[1025,16,128]{2,1,0:T(8,128)} %bitcast.10, s32[1,512]{1,0:T(1,128)} %bitcast.6), custom_call_target="tpu_custom_call" | custom-call | flops 3000000000 | bytes 6500000 | tf_op jit(solution)/shard_map/pack/pallas_call | solution.py:400
  7.9 7.3 %all-to-all-start = ((bf16[32,17,8,128]{3,2,1,0:T(8,128)(2,1)}), bf16[32,17,8,128]{3,2,1,0:T(8,128)(2,1)S(1)}, u32[]{:S(2)}, u32[]{:S(2)}) async-start(bf16[32,17,8,128]{3,2,1,0:T(8,128)(2,1)} %get-tuple-element.23), calls=%async_computation | async-start | bytes 2228224 | tf_op jit(solution)/shard_map/all_to_all | solution.py:421
  15.2 0.0 copy-start.8
  15.2 0.0 copy-start.7
  15.3 24.6 %fusion.3 = (bf16[8,1025,1025]{2,0,1:T(8,128)(2,1)}, bf16[8,1025,1025]{2,0,1:T(8,128)(2,1)}) fusion(bf16[16,1025,1025]{2,0,1:T(8,128)(2,1)} %param.6), kind=kLoop, calls=%fused_computation.7 | loop fusion | bytes 67240000 | tf_op jit(solution)/shard_map/slice | solution.py:419
  39.9 0.0 copy-done.8
  39.9 0.6 slice.23
  40.4 0.0 copy-done.7
  40.4 0.1 reshape.20
  40.6 0.7 broadcast_in_dim_reshape.6.rest_5_.rest_4_
  41.2 0.1 broadcast_in_dim_reshape.7
  41.3 18.3 %copy.15.rest_9_ = bf16[8,1025,1025]{2,1,0:T(8,128)(2,1)} copy(bf16[8,1025,1025]{2,0,1:T(8,128)(2,1)} %get-tuple-element.42) | data formatting | bytes 33620000 | tf_op jit(solution)/shard_map/optimization_barrier | solution.py:422
  59.6 0.7 fusion
  60.3 0.7 fusion.2
  61.0 0.3 broadcast_select_fusion
  61.3 0.9 pad.11.rest_8_.rest_7_
  62.2 7.9 %pack.3 = (bf16[32,17,8,128]{3,2,1,0:T(8,128)(2,1)}, bf16[32,16,8,128]{3,2,1,0:T(8,128)(2,1)}) custom-call(s32[512]{0:T(512)} %ord_ref.7, f32[3]{0:T(128)} %angle_ref.7, f32[1025,16,128]{2,1,0:T(8,128)} %bitcast.11, s32[1,512]{1,0:T(1,128)} %bitcast.7), custom_call_target="tpu_custom_call" | custom-call | flops 3000000000 | bytes 6500000 | tf_op jit(solution)/shard_map/pack/pallas_call | solution.py:400
  70.2 1.2 pad.10.rest_7_.rest_6_
  71.3 0.0 all-to-all-done.rest_0_
  71.3 5.8 %all-to-all-start.1 = ((bf16[32,17,8,128]{3,2,1,0:T(8,128)(2,1)}), bf16[32,17,8,128]{3,2,1,0:T(8,128)(2,1)S(1)}, u32[]{:S(2)}, u32[]{:S(2)}) async-start(bf16[32,17,8,128]{3,2,1,0:T(8,128)(2,1)} %get-tuple-element.25), calls=%async_computation.1 | async-start | bytes 2228224 | tf_op jit(solution)/shard_map/all_to_all | solution.py:423
  77.2 0.0 copy-start.5
  77.2 0.0 copy-start.6
  77.2 18.4 %copy.16.rest_8_ = bf16[8,1025,1025]{2,1,0:T(8,128)(2,1)} copy(bf16[8,1025,1025]{2,0,1:T(8,128)(2,1)} %get-tuple-element.41) | data formatting | bytes 33620000 | tf_op jit(solution)/shard_map/optimization_barrier | solution.py:426
  95.7 0.0 copy-done.5
  95.7 0.0 copy-done.6
  95.7 1.5 pad_maximum_fusion
  97.1 0.0 copy-done.3
  97.1 0.6 slice.28.rest_2_.rest_1_
  97.8 7.1 %all-to-all-done.1.rest_1_ = bf16[32,17,8,128]{3,2,1,0:T(8,128)(2,1)S(1)} async-done(((bf16[32,17,8,128]{3,2,1,0:T(8,128)(2,1)}), bf16[32,17,8,128]{3,2,1,0:T(8,128)(2,1)S(1)}, u32[]{:S(2)}, u32[]{:S(2)}) %all-to-all-start.1) | async-done | bytes 1114144 | tf_op jit(solution)/shard_map/all_to_all | solution.py:423
  104.8 0.7 slice.29.rest_3_.rest_2_
  105.5 0.3 copy-done.4
  105.8 3.6 %all-to-all-start.3 = ((bf16[32,32,8,128]{3,2,1,0:T(8,128)(2,1)}), bf16[32,32,8,128]{3,2,1,0:T(8,128)(2,1)S(1)}, u32[]{:S(2)}, u32[]{:S(2)}) async-start(bf16[32,32,8,128]{3,2,1,0:T(8,128)(2,1)} %pad_maximum_fusion), calls=%async_computation.3 | async-start | bytes 4194304 | tf_op jit(solution)/shard_map/all_to_all | solution.py:427
  109.5 0.8 dynamic_slice.3
  110.2 0.8 copy.13.rest_6_.rest_5_
  111.1 0.7 fusion.4
  111.7 0.7 broadcast_in_dim.44.rest_4_
  112.5 37.0 %degree.2 = (bf16[32,32,8,128]{3,2,1,0:T(8,128)(2,1)}, f32[512,128]{1,0:T(8,128)}) custom-call(s32[8]{0:T(128)} %get-tuple-element.44.deg_ref, bf16[32,17,8,128]{3,2,1,0:T(8,128)(2,1)} %copy-done.3, bf16[32,17,8,128]{3,2,1,0:T(8,128)(2,1)} %copy-done.4, bf16[32,1,8,128]{3,2,1,0:T(8,128)(2,1)} %slice.28.rest_2_.rest_1_, ...), custom_call_target="tpu_custom_call" | custom-call | flops 8000000000 | bytes 25000000 | tf_op jit(solution)/shard_map/degree/pallas_call | solution.py:439
  149.4 8.9 %all-to-all-done.3.rest_0_ = bf16[32,32,8,128]{3,2,1,0:T(8,128)(2,1)S(1)} async-done(((bf16[32,32,8,128]{3,2,1,0:T(8,128)(2,1)}), bf16[32,32,8,128]{3,2,1,0:T(8,128)(2,1)S(1)}, u32[]{:S(2)}, u32[]{:S(2)}) %all-to-all-start.3) | async-done | bytes 2097184 | tf_op jit(solution)/shard_map/all_to_all | solution.py:427
  158.4 1.3 copy-done.2
  159.7 4.0 %all-to-all-start.2 = ((bf16[32,32,8,128]{3,2,1,0:T(8,128)(2,1)}), bf16[32,32,8,128]{3,2,1,0:T(8,128)(2,1)S(1)}, u32[]{:S(2)}, u32[]{:S(2)}) async-start(bf16[32,32,8,128]{3,2,1,0:T(8,128)(2,1)} %get-tuple-element.35), calls=%async_computation.2 | async-start | bytes 4194304 | tf_op jit(solution)/shard_map/all_to_all | solution.py:462
  163.7 37.1 %degree.3 = (bf16[32,17,8,128]{3,2,1,0:T(8,128)(2,1)}, bf16[32,17,8,128]{3,2,1,0:T(8,128)(2,1)}) custom-call(s32[8]{0:T(128)} %get-tuple-element.43.deg_ref, bf16[32,32,8,128]{3,2,1,0:T(8,128)(2,1)} %copy-done.2, bf16[32,1,8,128]{3,2,1,0:T(8,128)(2,1)} %slice.28.rest_2_.rest_1_, bf16[32,1,8,128]{3,2,1,0:T(8,128)(2,1)} %slice.29.rest_3_.rest_2_, ...), custom_call_target="tpu_custom_call" | custom-call | flops 8000000000 | bytes 25000000 | tf_op jit(solution)/shard_map/degree/pallas_call | solution.py:439
  200.8 11.8 %all-to-all-done.2.rest_0_ = bf16[32,32,8,128]{3,2,1,0:T(8,128)(2,1)S(1)} async-done(((bf16[32,32,8,128]{3,2,1,0:T(8,128)(2,1)}), bf16[32,32,8,128]{3,2,1,0:T(8,128)(2,1)S(1)}, u32[]{:S(2)}, u32[]{:S(2)}) %all-to-all-start.2) | async-done | bytes 2097184 | tf_op jit(solution)/shard_map/all_to_all | solution.py:462
  212.6 33.5 %all_to_all.30.rest_1_ = bf16[32,17,8,128]{3,2,1,0:T(8,128)(2,1)} all-to-all(bf16[32,17,8,128]{3,2,1,0:T(8,128)(2,1)} %get-tuple-element.40), channel_id=1, replica_groups=mesh['grp'=1,'deg'=32] {'deg'}, dimensions={0} | all-to-all | bytes 2228224 | tf_op jit(solution)/shard_map/all_to_all | solution.py:462
  246.1 2.8 all-to-all-start.4
  248.9 9.7 %unpack.2.rest_2_ = f32[1025,16,128]{2,1,0:T(8,128)} custom-call(s32[512]{0:T(512)} %ord_ref.7, f32[3]{0:T(128)} %angle_ref.7, s32[1,512]{1,0:T(1,128)} %bitcast.8, bf16[32,32,8,128]{3,2,1,0:T(8,128)(2,1)} %copy-done, bf16[32,17,8,128]{3,2,1,0:T(8,128)(2,1)} %all_to_all.30.rest_1_), custom_call_target="tpu_custom_call" | custom-call | flops 3000000000 | bytes 6500000 | tf_op jit(solution)/shard_map/unpack/pallas_call | solution.py:466
  258.7 17.7 %all-to-all-done.4.rest_1_ = bf16[32,17,8,128]{3,2,1,0:T(8,128)(2,1)S(1)} async-done(((bf16[32,17,8,128]{3,2,1,0:T(8,128)(2,1)}), bf16[32,17,8,128]{3,2,1,0:T(8,128)(2,1)S(1)}, u32[]{:S(2)}, u32[]{:S(2)}) %all-to-all-start.4) | async-done | bytes 1114144 | tf_op jit(solution)/shard_map/all_to_all | solution.py:462
  276.4 1.0 copy-done.1
  277.4 9.7 %unpack.3 = f32[1025,16,128]{2,1,0:T(8,128)} custom-call(s32[512]{0:T(512)} %ord_ref.7, f32[3]{0:T(128)} %angle_ref.7, s32[1,512]{1,0:T(1,128)} %bitcast.9, bf16[32,32,8,128]{3,2,1,0:T(8,128)(2,1)} %copy-done, bf16[32,17,8,128]{3,2,1,0:T(8,128)(2,1)} %copy-done.1, f32[1025,16,128]{2,1,0:T(8,128)} %unpack.2.rest_2_), custom_call_target="tpu_custom_call", output_to_operand_aliasing={{}: (5, {})} | custom-call | flops 3000000000 | bytes 6500000 | tf_op jit(solution)/shard_map/unpack/pallas_call | solution.py:466
  (9 shorter events, 0.0 us)
Async XLA Ops:
  7.9 63.4 %all-to-all-start = ((bf16[32,17,8,128]{3,2,1,0:T(8,128)(2,1)}), bf16[32,17,8,128]{3,2,1,0:T(8,128)(2,1)S(1)}, u32[]{:S(2)}, u32[]{:S(2)}) async-start(bf16[32,17,8,128]{3,2,1,0:T(8,128)(2,1)} %get-tuple-element.23), calls=%async_computation | async-start | bytes 2228224 | tf_op jit(solution)/shard_map/all_to_all | solution.py:421
  15.2 24.6 %copy-start.8 = (f32[3]{0:T(128)S(1)}, f32[3]{0:T(128)}, u32[]{:S(2)}) copy-start(f32[3]{0:T(128)} %angle_ref.7) | copy-start | bytes 40
  15.2 25.2 %copy-start.7 = (s32[512]{0:T(512)S(1)}, s32[512]{0:T(512)}, u32[]{:S(2)}) copy-start(s32[512]{0:T(512)} %ord_ref.7) | copy-start | bytes 6148
  71.3 25.8 %copy-start.3 = (bf16[32,17,8,128]{3,2,1,0:T(8,128)(2,1)}, bf16[32,17,8,128]{3,2,1,0:T(8,128)(2,1)S(1)}, u32[]{:S(2)}) copy-start(bf16[32,17,8,128]{3,2,1,0:T(8,128)(2,1)S(1)} %all-to-all-done.rest_0_) | copy-start | bytes 3342340
  71.3 33.5 %all-to-all-start.1 = ((bf16[32,17,8,128]{3,2,1,0:T(8,128)(2,1)}), bf16[32,17,8,128]{3,2,1,0:T(8,128)(2,1)S(1)}, u32[]{:S(2)}, u32[]{:S(2)}) async-start(bf16[32,17,8,128]{3,2,1,0:T(8,128)(2,1)} %get-tuple-element.25), calls=%async_computation.1 | async-start | bytes 2228224 | tf_op jit(solution)/shard_map/all_to_all | solution.py:423
  77.2 18.5 %copy-start.5 = (bf16[32,16,8,128]{3,2,1,0:T(8,128)(2,1)S(1)}, bf16[32,16,8,128]{3,2,1,0:T(8,128)(2,1)}, u32[]{:S(2)}) copy-start(bf16[32,16,8,128]{3,2,1,0:T(8,128)(2,1)} %get-tuple-element.26) | copy-start | bytes 3145732
  77.2 18.5 %copy-start.6 = (bf16[32,16,8,128]{3,2,1,0:T(8,128)(2,1)S(1)}, bf16[32,16,8,128]{3,2,1,0:T(8,128)(2,1)}, u32[]{:S(2)}) copy-start(bf16[32,16,8,128]{3,2,1,0:T(8,128)(2,1)} %get-tuple-element.27) | copy-start | bytes 3145732
  104.8 1.0 copy-start.4
  105.8 52.5 %all-to-all-start.3 = ((bf16[32,32,8,128]{3,2,1,0:T(8,128)(2,1)}), bf16[32,32,8,128]{3,2,1,0:T(8,128)(2,1)S(1)}, u32[]{:S(2)}, u32[]{:S(2)}) async-start(bf16[32,32,8,128]{3,2,1,0:T(8,128)(2,1)} %pad_maximum_fusion), calls=%async_computation.3 | async-start | bytes 4194304 | tf_op jit(solution)/shard_map/all_to_all | solution.py:427
  158.4 1.3 copy-start.2
  159.7 52.9 %all-to-all-start.2 = ((bf16[32,32,8,128]{3,2,1,0:T(8,128)(2,1)}), bf16[32,32,8,128]{3,2,1,0:T(8,128)(2,1)S(1)}, u32[]{:S(2)}, u32[]{:S(2)}) async-start(bf16[32,32,8,128]{3,2,1,0:T(8,128)(2,1)} %get-tuple-element.35), calls=%async_computation.2 | async-start | bytes 4194304 | tf_op jit(solution)/shard_map/all_to_all | solution.py:462
  212.6 33.5 %copy-start = (bf16[32,32,8,128]{3,2,1,0:T(8,128)(2,1)}, bf16[32,32,8,128]{3,2,1,0:T(8,128)(2,1)S(1)}, u32[]{:S(2)}) copy-start(bf16[32,32,8,128]{3,2,1,0:T(8,128)(2,1)S(1)} %all-to-all-done.2.rest_0_) | copy-start | bytes 6291460
  246.1 30.3 %all-to-all-start.4 = ((bf16[32,17,8,128]{3,2,1,0:T(8,128)(2,1)}), bf16[32,17,8,128]{3,2,1,0:T(8,128)(2,1)S(1)}, u32[]{:S(2)}, u32[]{:S(2)}) async-start(bf16[32,17,8,128]{3,2,1,0:T(8,128)(2,1)} %get-tuple-element.39), calls=%async_computation.4 | async-start | bytes 2228224 | tf_op jit(solution)/shard_map/all_to_all | solution.py:462
  276.4 1.0 copy-start.1

commit v4 on v3

--- a/solution.py
+++ b/solution.py
@@ -410,20 +410,19 @@
         for h in range(halves)
     ]
     swap = functools.partial(lax.all_to_all, axis_name="deg", split_axis=0, concat_axis=0, tiled=True)
+    first, tilt, sorted_orders = lax.optimization_barrier((sends[0][0], angles[1], order_pairs))
     ct, st = (
-        jnp.pad(t, ((pairs, 7), (0, 0))) for t in phases(jnp.arange(width, dtype=jnp.int32), angles[1])
-    )
-    by_part = jnp.transpose(order_pairs.reshape(devices, halves, part), (1, 0, 2)).reshape(-1)
+        jnp.pad(t, ((pairs, 7), (0, 0))) for t in phases(jnp.arange(width, dtype=jnp.int32), tilt)
+    )
+    by_part = jnp.transpose(sorted_orders.reshape(devices, halves, part), (1, 0, 2)).reshape(-1)
     prow, pcol = by_part[None, :], by_part[:, None]
-    tabled = [
-        with_layout_constraint(tables[k * each : (k + 1) * each], Layout((0, 1, 2))) for k in range(chunks)
-    ]
-    arrived = [[swap(sends[0][0])]]
-    early, tabled[0], ct, st, prow, pcol = lax.optimization_barrier((sends[1][0], tabled[0], ct, st, prow, pcol))
+    tables = with_layout_constraint(tables, Layout((0, 1, 2)))
+    arrived = [[swap(first)]]
+    early, ct, st, prow, pcol = lax.optimization_barrier((sends[1][0], ct, st, prow, pcol))
     arrived[0].append(swap(early))
     extra_in = [a[:, 2 * each :] for a in arrived[0]]
     later = jnp.concatenate([sends[h][1] for h in range(halves)], 1)
-    later, tabled[1], extra_in = lax.optimization_barrier((later, tabled[1], extra_in))
+    later, tables, extra_in = lax.optimization_barrier((later, tables, extra_in))
     arrived.append([swap(later)])
     extra_back = jnp.zeros((pairs, 128), F32)
     homes = []
@@ -446,7 +445,7 @@
                 in_specs=[full(a.shape) for a in arrived[k]]
                 + [full((devices, 1, part, 128))] * halves
                 + [full((pairs, 128)), full((1, pairs)), full((pairs, 1)), full(ct.shape), full(st.shape)]
-                + [pl.BlockSpec((None, width, width), lambda c, deg: (c, 0, 0))],
+                + [pl.BlockSpec((None, width, width), lambda c, deg, k=k: (k * each + c, 0, 0))],
                 out_specs=out_specs,
                 scratch_shapes=[square] * 4
                 + [pltpu.VMEM((3 * pairs + 16, 128), F32), pltpu.VMEM((pairs, 128), F32)],
@@ -455,7 +454,7 @@
             cost_estimate=cost(16 * 10**9 // chunks, 50 * 10**6 // chunks),
         )(
             my_degrees[k * each : (k + 1) * each], *arrived[k], *extra_in,
-            extra_back, prow, pcol, ct, st, tabled[k],
+            extra_back, prow, pcol, ct, st, tables,
         )
         if not last:
             extra_back = done[sent]

time: 288 us -> 263 us (0.913)
  local copies, waits for them, and re-layouts: 71.8 us -> 37.3 us
  waiting for transfers between devices: 45.5 us -> 53.7 us
    optimization_barrier x3 -> x1, local copies, waits for them, and re-layouts: 37.6 us -> 0.88 us  [shards(): lax.optimization_barrier((sends[1][0], ct, st, prow, pcol))]
    unnamed x18 -> x15, local copies, waits for them, and re-layouts: 2.7 us -> 28.8 us
    slice x1 -> x0, local copies, waits for them, and re-layouts: 24.6 us -> none  [shards(): tables[k * each:(k + 1) * each]]
    all_to_all x1, waiting for transfers between devices: 0.01 us -> 15.1 us  [shards(): arrived = [[swap(first)]]]
    all_to_all x1, waiting for transfers between devices: 7.06 us -> 0.01 us  [shards(): arrived[0].append(swap(early))]
  transfers between devices with their start and end apart: 5 -> 5, of which waited for: 4 -> 4; matrix products, arithmetic and copies ran while one was open for 25% -> 14% of each run, Pallas kernels for 32% -> 35%
where the time goes in v4:
time: 263 us; the launch traced here: 262 us
  Pallas kernels  109 us (41%)
  waiting for transfers between devices  53.7 us (20%)
  local copies, waits for them, and re-layouts  37.3 us (14%)
  blocking collectives  33.5 us (13%)
  starting transfers between devices  23.6 us (9%)
  other arithmetic  4.32 us (2%)
    pallas_call x2, Pallas kernels, shards(): pl.pallas_call(functools.partial(degree_kernel, halves, pairs, each, last...  73.9 us
    all_to_all x1, blocking collectives, shards(): homes.append([swap(d) for d in done[:sent]])  33.5 us
    all_to_all x2, waiting for transfers between devices, shards(): homes.append([swap(d) for d in done[:sent]])  29.6 us
    unnamed x15, local copies, waits for them, and re-layouts  28.8 us
    pallas_call x2, Pallas kernels, shards(): pl.pallas_call(functools.partial(unpack_kernel, h, local, pairs, chunks),...  19.5 us
    pallas_call x2, Pallas kernels, shards(): pl.pallas_call(functools.partial(pack_kernel, h, local, pairs, chunks), n...  15.8 us
    all_to_all x1, waiting for transfers between devices, shards(): arrived = [[swap(first)]]  15.1 us
    all_to_all x1, waiting for transfers between devices, shards(): arrived.append([swap(later)])  8.96 us
  transfers between devices with their start and end apart: 5, of which 4 were waited for; matrix products, arithmetic and copies ran while one was open for 14% of the time, Pallas kernels for 35%

profile of v4, /device:TPU:0, one launch (start us, length us, event | category | flops | bytes accessed | tf_op | source)
XLA Modules:
  0.0 261.9 jit_solution(11152054636390589518)
XLA Ops:
  0.0 1.2 slice.16
  1.2 7.9 %pack.2 = (bf16[32,17,8,128]{3,2,1,0:T(8,128)(2,1)}, bf16[32,16,8,128]{3,2,1,0:T(8,128)(2,1)}) custom-call(s32[512]{0:T(512)} %ord_ref.7, f32[3]{0:T(128)} %angle_ref.7, f32[1025,16,128]{2,1,0:T(8,128)} %bitcast.10, s32[1,512]{1,0:T(1,128)} %bitcast.6), custom_call_target="tpu_custom_call" | custom-call | flops 3000000000 | bytes 6500000 | tf_op jit(solution)/shard_map/pack/pallas_call | solution.py:400
  9.2 0.0 copy-start.6
  9.2 7.3 %all-to-all-start = ((bf16[32,17,8,128]{3,2,1,0:T(8,128)(2,1)}), bf16[32,17,8,128]{3,2,1,0:T(8,128)(2,1)S(1)}, u32[]{:S(2)}, u32[]{:S(2)}) async-start(bf16[32,17,8,128]{3,2,1,0:T(8,128)(2,1)} %get-tuple-element.26), calls=%async_computation | async-start | bytes 2228224 | tf_op jit(solution)/shard_map/all_to_all | solution.py:420
  16.5 0.0 copy-done.6
  16.5 0.1 reshape.20
  16.6 0.1 broadcast_in_dim_reshape.7
  16.7 0.7 broadcast_in_dim_reshape.6.rest_5_.rest_4_
  17.4 0.6 fusion
  18.0 0.6 fusion.2
  18.7 0.3 broadcast_select_fusion
  19.0 1.0 pad.11.rest_8_.rest_7_
  20.0 7.9 %pack.3 = (bf16[32,17,8,128]{3,2,1,0:T(8,128)(2,1)}, bf16[32,16,8,128]{3,2,1,0:T(8,128)(2,1)}) custom-call(s32[512]{0:T(512)} %ord_ref.7, f32[3]{0:T(128)} %angle_ref.7, f32[1025,16,128]{2,1,0:T(8,128)} %bitcast.11, s32[1,512]{1,0:T(1,128)} %bitcast.7), custom_call_target="tpu_custom_call" | custom-call | flops 3000000000 | bytes 6500000 | tf_op jit(solution)/shard_map/pack/pallas_call | solution.py:400
  27.9 1.1 pad.10.rest_7_.rest_6_
  29.0 15.1 %all-to-all-done.rest_0_ = bf16[32,17,8,128]{3,2,1,0:T(8,128)(2,1)S(1)} async-done(((bf16[32,17,8,128]{3,2,1,0:T(8,128)(2,1)}), bf16[32,17,8,128]{3,2,1,0:T(8,128)(2,1)S(1)}, u32[]{:S(2)}, u32[]{:S(2)}) %all-to-all-start) | async-done | bytes 1114144 | tf_op jit(solution)/shard_map/all_to_all | solution.py:420
  44.1 0.0 copy-start.2
  44.1 3.6 %all-to-all-start.1 = ((bf16[32,17,8,128]{3,2,1,0:T(8,128)(2,1)}), bf16[32,17,8,128]{3,2,1,0:T(8,128)(2,1)S(1)}, u32[]{:S(2)}, u32[]{:S(2)}) async-start(bf16[32,17,8,128]{3,2,1,0:T(8,128)(2,1)} %get-tuple-element.30), calls=%async_computation.1 | async-start | bytes 2228224 | tf_op jit(solution)/shard_map/all_to_all | solution.py:422
  47.8 0.0 copy-start.5
  47.8 26.1 %copy.10.rest_9_.rest_8_ = bf16[16,1025,1025]{2,1,0:T(8,128)(2,1)} copy(bf16[16,1025,1025]{2,0,1:T(8,128)(2,1)} %param.6) | data formatting | bytes 67240000 | tf_op args[1]
  73.8 0.0 copy-done.5
  73.8 2.7 %pad_maximum_fusion = bf16[32,32,8,128]{3,2,1,0:T(8,128)(2,1)} fusion(bf16[32,16,8,128]{3,2,1,0:T(8,128)(2,1)} %get-tuple-element.32, bf16[32,16,8,128]{3,2,1,0:T(8,128)(2,1)S(1)} %copy-done.5), kind=kLoop, calls=%fused_computation | loop fusion | flops 1048576 | bytes 4194304 | tf_op jit(solution)/shard_map/concatenate | solution.py:424
  76.6 0.0 copy-done.2
  76.6 0.6 slice.20.rest_2_.rest_1_
  77.2 0.0 all-to-all-done.1.rest_1_
  77.2 0.0 copy-start.3
  77.2 0.7 slice.21.rest_3_.rest_2_
  77.9 0.4 copy-done.3
  78.3 5.8 %all-to-all-start.3 = ((bf16[32,32,8,128]{3,2,1,0:T(8,128)(2,1)}), bf16[32,32,8,128]{3,2,1,0:T(8,128)(2,1)S(1)}, u32[]{:S(2)}, u32[]{:S(2)}) async-start(bf16[32,32,8,128]{3,2,1,0:T(8,128)(2,1)} %pad_maximum_fusion), calls=%async_computation.3 | async-start | bytes 4194304 | tf_op jit(solution)/shard_map/all_to_all | solution.py:426
  84.1 0.8 dynamic_slice.3
  84.9 0.9 copy.11.rest_6_.rest_5_
  85.7 0.6 fusion.3
  86.3 0.7 broadcast_in_dim.44.rest_4_
  87.1 37.0 %degree.2 = (bf16[32,32,8,128]{3,2,1,0:T(8,128)(2,1)}, f32[512,128]{1,0:T(8,128)}) custom-call(s32[8]{0:T(128)} %get-tuple-element.46.deg_ref, bf16[32,17,8,128]{3,2,1,0:T(8,128)(2,1)} %copy-done.2, bf16[32,17,8,128]{3,2,1,0:T(8,128)(2,1)} %copy-done.3, bf16[32,1,8,128]{3,2,1,0:T(8,128)(2,1)} %slice.20.rest_2_.rest_1_, ...), custom_call_target="tpu_custom_call" | custom-call | flops 8000000000 | bytes 25000000 | tf_op jit(solution)/shard_map/degree/pallas_call | solution.py:438
  124.0 9.0 %all-to-all-done.3.rest_0_ = bf16[32,32,8,128]{3,2,1,0:T(8,128)(2,1)S(1)} async-done(((bf16[32,32,8,128]{3,2,1,0:T(8,128)(2,1)}), bf16[32,32,8,128]{3,2,1,0:T(8,128)(2,1)S(1)}, u32[]{:S(2)}, u32[]{:S(2)}) %all-to-all-start.3) | async-done | bytes 2097184 | tf_op jit(solution)/shard_map/all_to_all | solution.py:426
  133.0 0.0 copy-start.1
  133.0 1.3 copy-done.1
  134.3 4.0 %all-to-all-start.2 = ((bf16[32,32,8,128]{3,2,1,0:T(8,128)(2,1)}), bf16[32,32,8,128]{3,2,1,0:T(8,128)(2,1)S(1)}, u32[]{:S(2)}, u32[]{:S(2)}) async-start(bf16[32,32,8,128]{3,2,1,0:T(8,128)(2,1)} %get-tuple-element.40), calls=%async_computation.2 | async-start | bytes 4194304 | tf_op jit(solution)/shard_map/all_to_all | solution.py:461
  138.3 37.0 %degree.3 = (bf16[32,17,8,128]{3,2,1,0:T(8,128)(2,1)}, bf16[32,17,8,128]{3,2,1,0:T(8,128)(2,1)}) custom-call(s32[8]{0:T(128)} %get-tuple-element.45.deg_ref, bf16[32,32,8,128]{3,2,1,0:T(8,128)(2,1)} %copy-done.1, bf16[32,1,8,128]{3,2,1,0:T(8,128)(2,1)} %slice.20.rest_2_.rest_1_, bf16[32,1,8,128]{3,2,1,0:T(8,128)(2,1)} %slice.21.rest_3_.rest_2_, ...), custom_call_target="tpu_custom_call" | custom-call | flops 8000000000 | bytes 25000000 | tf_op jit(solution)/shard_map/degree/pallas_call | solution.py:438
  175.3 11.9 %all-to-all-done.2.rest_0_ = bf16[32,32,8,128]{3,2,1,0:T(8,128)(2,1)S(1)} async-done(((bf16[32,32,8,128]{3,2,1,0:T(8,128)(2,1)}), bf16[32,32,8,128]{3,2,1,0:T(8,128)(2,1)S(1)}, u32[]{:S(2)}, u32[]{:S(2)}) %all-to-all-start.2) | async-done | bytes 2097184 | tf_op jit(solution)/shard_map/all_to_all | solution.py:461
  187.2 0.0 copy-start
  187.2 33.5 %all_to_all.30.rest_1_ = bf16[32,17,8,128]{3,2,1,0:T(8,128)(2,1)} all-to-all(bf16[32,17,8,128]{3,2,1,0:T(8,128)(2,1)} %get-tuple-element.44), channel_id=1, replica_groups=mesh['grp'=1,'deg'=32] {'deg'}, dimensions={0} | all-to-all | bytes 2228224 | tf_op jit(solution)/shard_map/all_to_all | solution.py:461
  220.7 0.0 copy-done
  220.7 2.8 %all-to-all-start.4 = ((bf16[32,17,8,128]{3,2,1,0:T(8,128)(2,1)}), bf16[32,17,8,128]{3,2,1,0:T(8,128)(2,1)S(1)}, u32[]{:S(2)}, u32[]{:S(2)}) async-start(bf16[32,17,8,128]{3,2,1,0:T(8,128)(2,1)} %get-tuple-element.43), calls=%async_computation.4 | async-start | bytes 2228224 | tf_op jit(solution)/shard_map/all_to_all | solution.py:461
  223.6 9.7 %unpack.2.rest_2_ = f32[1025,16,128]{2,1,0:T(8,128)} custom-call(s32[512]{0:T(512)} %ord_ref.7, f32[3]{0:T(128)} %angle_ref.7, s32[1,512]{1,0:T(1,128)} %bitcast.8, bf16[32,32,8,128]{3,2,1,0:T(8,128)(2,1)} %copy-done, bf16[32,17,8,128]{3,2,1,0:T(8,128)(2,1)} %all_to_all.30.rest_1_), custom_call_target="tpu_custom_call" | custom-call | flops 3000000000 | bytes 6500000 | tf_op jit(solution)/shard_map/unpack/pallas_call | solution.py:465
  233.3 17.7 %all-to-all-done.4.rest_1_ = bf16[32,17,8,128]{3,2,1,0:T(8,128)(2,1)S(1)} async-done(((bf16[32,17,8,128]{3,2,1,0:T(8,128)(2,1)}), bf16[32,17,8,128]{3,2,1,0:T(8,128)(2,1)S(1)}, u32[]{:S(2)}, u32[]{:S(2)}) %all-to-all-start.4) | async-done | bytes 1114144 | tf_op jit(solution)/shard_map/all_to_all | solution.py:461
  251.0 0.0 copy-start.4
  251.0 1.0 copy-done.4
  252.0 9.7 %unpack.3 = f32[1025,16,128]{2,1,0:T(8,128)} custom-call(s32[512]{0:T(512)} %ord_ref.7, f32[3]{0:T(128)} %angle_ref.7, s32[1,512]{1,0:T(1,128)} %bitcast.9, bf16[32,32,8,128]{3,2,1,0:T(8,128)(2,1)} %copy-done, bf16[32,17,8,128]{3,2,1,0:T(8,128)(2,1)} %copy-done.4, f32[1025,16,128]{2,1,0:T(8,128)} %unpack.2.rest_2_), custom_call_target="tpu_custom_call", output_to_operand_aliasing={{}: (5, {})} | custom-call | flops 3000000000 | bytes 6500000 | tf_op jit(solution)/shard_map/unpack/pallas_call | solution.py:465
  (3 shorter events, 0.0 us)
Async XLA Ops:
  9.2 7.3 %copy-start.6 = (s32[512]{0:T(512)S(1)}, s32[512]{0:T(512)}, u32[]{:S(2)}) copy-start(s32[512]{0:T(512)} %ord_ref.7) | copy-start | bytes 6148
  9.2 35.0 %all-to-all-start = ((bf16[32,17,8,128]{3,2,1,0:T(8,128)(2,1)}), bf16[32,17,8,128]{3,2,1,0:T(8,128)(2,1)S(1)}, u32[]{:S(2)}, u32[]{:S(2)}) async-start(bf16[32,17,8,128]{3,2,1,0:T(8,128)(2,1)} %get-tuple-element.26), calls=%async_computation | async-start | bytes 2228224 | tf_op jit(solution)/shard_map/all_to_all | solution.py:420
  44.1 32.5 %copy-start.2 = (bf16[32,17,8,128]{3,2,1,0:T(8,128)(2,1)}, bf16[32,17,8,128]{3,2,1,0:T(8,128)(2,1)S(1)}, u32[]{:S(2)}) copy-start(bf16[32,17,8,128]{3,2,1,0:T(8,128)(2,1)S(1)} %all-to-all-done.rest_0_) | copy-start | bytes 3342340
  44.1 33.1 %all-to-all-start.1 = ((bf16[32,17,8,128]{3,2,1,0:T(8,128)(2,1)}), bf16[32,17,8,128]{3,2,1,0:T(8,128)(2,1)S(1)}, u32[]{:S(2)}, u32[]{:S(2)}) async-start(bf16[32,17,8,128]{3,2,1,0:T(8,128)(2,1)} %get-tuple-element.30), calls=%async_computation.1 | async-start | bytes 2228224 | tf_op jit(solution)/shard_map/all_to_all | solution.py:422
  47.8 26.1 %copy-start.5 = (bf16[32,16,8,128]{3,2,1,0:T(8,128)(2,1)S(1)}, bf16[32,16,8,128]{3,2,1,0:T(8,128)(2,1)}, u32[]{:S(2)}) copy-start(bf16[32,16,8,128]{3,2,1,0:T(8,128)(2,1)} %get-tuple-element.31) | copy-start | bytes 3145732
  77.2 1.1 copy-start.3
  78.3 54.7 %all-to-all-start.3 = ((bf16[32,32,8,128]{3,2,1,0:T(8,128)(2,1)}), bf16[32,32,8,128]{3,2,1,0:T(8,128)(2,1)S(1)}, u32[]{:S(2)}, u32[]{:S(2)}) async-start(bf16[32,32,8,128]{3,2,1,0:T(8,128)(2,1)} %pad_maximum_fusion), calls=%async_computation.3 | async-start | bytes 4194304 | tf_op jit(solution)/shard_map/all_to_all | solution.py:426
  133.0 1.3 copy-start.1
  134.3 52.9 %all-to-all-start.2 = ((bf16[32,32,8,128]{3,2,1,0:T(8,128)(2,1)}), bf16[32,32,8,128]{3,2,1,0:T(8,128)(2,1)S(1)}, u32[]{:S(2)}, u32[]{:S(2)}) async-start(bf16[32,32,8,128]{3,2,1,0:T(8,128)(2,1)} %get-tuple-element.40), calls=%async_computation.2 | async-start | bytes 4194304 | tf_op jit(solution)/shard_map/all_to_all | solution.py:461
  187.2 33.5 %copy-start = (bf16[32,32,8,128]{3,2,1,0:T(8,128)(2,1)}, bf16[32,32,8,128]{3,2,1,0:T(8,128)(2,1)S(1)}, u32[]{:S(2)}) copy-start(bf16[32,32,8,128]{3,2,1,0:T(8,128)(2,1)S(1)} %all-to-all-done.2.rest_0_) | copy-start | bytes 6291460
  220.7 30.3 %all-to-all-start.4 = ((bf16[32,17,8,128]{3,2,1,0:T(8,128)(2,1)}), bf16[32,17,8,128]{3,2,1,0:T(8,128)(2,1)S(1)}, u32[]{:S(2)}, u32[]{:S(2)}) async-start(bf16[32,17,8,128]{3,2,1,0:T(8,128)(2,1)} %get-tuple-element.43), calls=%async_computation.4 | async-start | bytes 2228224 | tf_op jit(solution)/shard_map/all_to_all | solution.py:461
  251.0 1.0 copy-start.4
